TPU v7x, 512 devices: a whole 4x4x16 slice. The times are simulated.
512 devices in a mesh: grp: 16 (over z), cube: 32 (over y, x, core).
Axes of the slice: x: 4, y: 4, z: 16, core: 2. Of those that a mesh axis runs over, the one named last changes fastest.
Arguments:
- density: float32 [16, 32, 64, 512], P('grp', 'cube'), may hold values from 0.5 to 2
- momentum: float32 [16, 32, 3, 64, 512], P('grp', 'cube'), may hold values from -3 to 3
- element_size: float32 [16, 32, 3, 64], P('grp', 'cube'), may hold values from 0.5 to 2
- section_slots: int32 [16, 32, 5, 1024], P('grp', 'cube'), may hold values from 0 to 28671, as said below
- section_counts: int32 [16, 32, 5], P('grp', 'cube'), may hold values from 512 to 1024, as said below
- cross_slots: int32 [16, 32, 2, 1024], P('grp', 'cube'), may hold values from 0 to 28671, as said below
- cross_counts: int32 [16, 32, 2], P('grp', 'cube'), may hold values from 512 to 1024, as said below
Outputs:
- new_density: float32 [16, 32, 64, 512], P('grp', 'cube')
- new_momentum: float32 [16, 32, 3, 64, 512], P('grp', 'cube')
Inputs may be any that keep to these rules, and one draw needn't show every extreme that they name: All slots of a device, of section_slots and cross_slots together, name different nodes. `section_counts`: the two devices of a pair have the same count for that bit; some pair fills all 1024 slots. All slots of a device, of section_slots and cross_slots together, name different nodes. `cross_counts`: a device's count toward the upper group equals the upper device's count toward the lower group; some pair fills all 1024 slots.
All inputs are finite; a program needn't handle non-finite values.
Results may differ from a plain program's by a relative error of at most 0.0003.
Values sent between devices are 32-bit elements; how exact they have to be, the bound alone decides.
No kernel may reach another device: no remote copies, remote signals or barrier semaphores. Data moves between devices by JAX's collectives and lax.ppermute only.
A program may use at most 64 MiB of HBM per device.

v0:
```python
import jax
import jax.numpy as jnp
import numpy as np
from jax import lax
from jax.experimental import pallas as pl
from jax.experimental.pallas import tpu as pltpu
from jax.sharding import PartitionSpec as P

GAMMA = 1.4
DT = 0.01
ORDER = 7
COLS = 448
F32 = jnp.float32
BF16 = jnp.bfloat16


def gll_tables():
    points = np.array(
        [
            -1.0,
            -0.8717401485096066,
            -0.5917001814331423,
            -0.2092992179024789,
            0.2092992179024789,
            0.5917001814331423,
            0.8717401485096066,
            1.0,
        ]
    )
    weights = np.array(
        [
            1.0 / 28.0,
            0.2107042271435061,
            0.3411226924835044,
            0.4124587946587038,
            0.4124587946587038,
            0.3411226924835044,
            0.2107042271435061,
            1.0 / 28.0,
        ]
    )
    previous = np.ones(8)
    current = points.copy()
    for order_now in range(1, ORDER):
        following = ((2 * order_now + 1) * points * current - order_now * previous) / (
            order_now + 1
        )
        previous = current
        current = following
    derivative = np.zeros((8, 8))
    for i in range(8):
        for j in range(8):
            if i != j:
                derivative[i, j] = current[i] / (current[j] * (points[i] - points[j]))
    derivative[0, 0] = -ORDER * (ORDER + 1) / 4.0
    derivative[7, 7] = ORDER * (ORDER + 1) / 4.0
    return (points, weights, derivative)


def bf16_parts(table, count):
    rest = np.asarray(table, np.float32)
    parts = []
    for _ in range(count):
        part = rest.astype(BF16)
        parts.append(part)
        rest = rest - part.astype(np.float32)
    return parts


def tables():
    _, weights, derivative = gll_tables()
    along_first = np.kron(derivative, np.eye(64)).T
    along_second = np.kron(np.eye(4), np.kron(derivative, np.eye(8))).T
    along_third = np.kron(np.eye(32), derivative).T
    first = np.stack(bf16_parts(along_first, 2))
    inner = np.stack(bf16_parts(along_second, 2) + bf16_parts(along_third, 2))
    node = np.kron(weights, np.kron(weights, weights)).astype(np.float32)[None]
    node_parts = np.concatenate(
        bf16_parts(node, 3) + [np.zeros((13, 512), np.float32).astype(BF16)], axis=0
    )
    return first, inner, node, node_parts


def split(value):
    high = value.astype(BF16)
    low = (value - high.astype(F32)).astype(BF16)
    return high, low


def element_and_column(ids):
    element = lax.shift_right_logical(lax.shift_right_logical(ids, 6) * 9363, 16)
    return element, ids - element * COLS


def column_onehot(column):
    rows = lax.broadcasted_iota(jnp.int32, (512, column.shape[1]), 0)
    return jnp.where(rows == column, 1.0, 0.0).astype(BF16)


def element_mask(element):
    rows = lax.broadcasted_iota(jnp.int32, (64, element.shape[1]), 0)
    return rows == element


def as_column(row):
    shape = (64, 64)
    same = lax.broadcasted_iota(jnp.int32, shape, 0) == lax.broadcasted_iota(jnp.int32, shape, 1)
    return jnp.sum(jnp.where(same, row, 0.0), axis=1, keepdims=True)


def low_lanes(shape):
    return lax.broadcasted_iota(jnp.int32, shape, 1) < 64


def dot(a, b):
    return jnp.dot(a, b, preferred_element_type=F32)


def pick(table, volumes, ids, count, send, at):
    element, column = element_and_column(ids)
    picked = dot(table[...], column_onehot(column))
    mask = element_mask(element)
    live = lax.broadcasted_iota(jnp.int32, ids.shape, 1) < count
    volume = jnp.where(mask, volumes[0, :, :1], 0.0)
    face_volume = jnp.where(jnp.logical_and(mask, column < 64), volumes[1, :, :1], 0.0)
    volume = jnp.sum(volume + face_volume, axis=0, keepdims=True)
    rows = []
    for f in range(4):
        row = picked[64 * f : 64 * f + 64] + picked[64 * f + 256 : 64 * f + 320]
        rows.append(jnp.sum(jnp.where(mask, row, 0.0), axis=0, keepdims=True))
    rows.append(volume * (picked[512:513] + picked[513:514] + picked[514:515]))
    for f in range(5):
        row = jnp.where(live, rows[f], 0.0)
        for t in range(8):
            send[at, f, t : t + 1, :] = row[:, 128 * t : 128 * t + 128]


def spread(ids, count, own, got):
    at = lax.broadcasted_iota(jnp.int32, (8, 128), 0) * 128
    live = at + lax.broadcasted_iota(jnp.int32, (8, 128), 1) < count
    before = DT / own[4]
    after = DT / (own[4] + got[4])
    parts = []
    for f in range(4):
        change = (own[f] + got[f]) * after - own[f] * before
        parts.append(split(jnp.where(live, change, 0.0)))
    element, column = element_and_column(ids)
    mask = element_mask(element)
    rows = []
    for p in range(2):
        for f in range(4):
            part = parts[f][p].astype(F32)
            row = jnp.concatenate([part[t : t + 1, :] for t in range(8)], axis=1)
            rows.append(jnp.where(mask, row, 0.0).astype(BF16))
    added = lax.dot_general(
        jnp.concatenate(rows, axis=0), column_onehot(column), (((1,), (1,)), ((), ())),
        preferred_element_type=F32,
    )
    return added[:256] + added[256:]


def carried(side, section, cross, arriving):
    lower = side == (0 if arriving else 1)
    return [
        section[2 + 2 * side],
        section[1 + 2 * side],
        jnp.where(lower, cross[0:1, :], cross[1:2, :]),
    ]


def carried_counts(side, section_n, cross_n, arriving):
    lower = side == (0 if arriving else 1)
    return [
        section_n[2 + 2 * side],
        section_n[1 + 2 * side],
        jnp.where(lower, cross_n[0], cross_n[1]),
    ]


def sums_kernel(
    density, momentum, sizes, first, inner, node, node_parts, section, cross, section_n, cross_n,
    core, steps, table, volumes, send,
):
    rho = density[...]
    inverse = 1.0 / rho
    mom = [momentum[a] for a in range(3)]
    velocity = [m * inverse for m in mom]
    pressure = jnp.exp(GAMMA * jnp.log(rho))
    h = [as_column(sizes[d]) for d in range(3)]
    scale = [h[1] * h[2] * 0.25, h[0] * h[2] * 0.25, h[0] * h[1] * 0.25]
    jacobian = h[0] * h[1] * h[2] * 0.125

    def flux(d):
        parts = [mom[d]]
        for a in range(3):
            part = mom[a] * velocity[d]
            parts.append(part + pressure if a == d else part)
        return split(jnp.concatenate([part * scale[d] for part in parts], axis=0))

    high, low = flux(0)
    change = dot(high, first[0]) + dot(low, first[0]) + dot(high, first[1])
    halves = [change[:, :256], change[:, 256:]]
    for d in (1, 2):
        high, low = flux(d)
        big, small = inner[2 * d - 2], inner[2 * d - 1]
        for k in range(2):
            lanes = slice(256 * k, 256 * k + 256)
            halves[k] += dot(high[:, lanes], big) + dot(low[:, lanes], big)
            halves[k] += dot(high[:, lanes], small)
    change = jnp.concatenate(halves, axis=1)
    node_w = node[...]

    def with_face(value):
        face = pltpu.roll(pltpu.roll(value[:, 384:], 64, 1), 1, 0)
        head = value[:, :128] + jnp.where(low_lanes((64, 128)), face, 0.0)
        return jnp.concatenate([head, value[:, 128:]], axis=1)

    share = DT / with_face(jacobian * node_w)
    for f in range(4):
        value = with_face(-change[64 * f : 64 * f + 64] * node_w)
        steps[f] = value * share
        high, low = split(value)
        table[64 * f : 64 * f + 64, :] = high
        table[64 * f + 256 : 64 * f + 320, :] = low
    table[512:528, :] = node_parts[...]
    volumes[0] = jnp.broadcast_to(jacobian, (64, 128))
    volumes[1] = pltpu.roll(volumes[0], 1, 0)

    pick(table, volumes, section[0], section_n[0], send, 0)
    ids = carried(1 - core[0], section, cross, False)
    counts = carried_counts(1 - core[0], section_n, cross_n, False)
    for j in range(3):
        pick(table, volumes, ids[j], counts[j], send, j + 1)


def gather_kernel(table, volumes, section, cross, section_n, cross_n, core, send):
    ids = carried(core[0], section, cross, False)
    counts = carried_counts(core[0], section_n, cross_n, False)
    for j in range(3):
        pick(table, volumes, ids[j], counts[j], send, j)


def pack_kernel(far_a, far_b, far_c, back):
    for j, far in enumerate((far_a, far_b, far_c)):
        back[j] = far[1]


def scatter_kernel(
    steps, section, cross, section_n, cross_n, core, sent, own, shared, far_a, far_b, far_c, total
):
    side = core[0]
    ids = carried(side, section, cross, True)
    counts = carried_counts(side, section_n, cross_n, True)
    added = spread(section[0], section_n[0], sent[0], shared[0])
    mine = (own[0], own[1], sent[3])
    for j, far in enumerate((far_a, far_b, far_c)):
        added += spread(ids[j], counts[j], mine[j], far[0])
    for f in range(4):
        total[f] = steps[f] + added[64 * f : 64 * f + 64]


def update_kernel(
    density, momentum, total, section, cross, section_n, cross_n, core, sent, own, relayed,
    new_density, new_momentum, ready, arrived,
):
    side = 1 - core[0]
    ids = carried(side, section, cross, True)
    counts = carried_counts(side, section_n, cross_n, True)
    mine = (sent[1], sent[2], own[2])
    added = None
    for j in range(3):
        more = spread(ids[j], counts[j], mine[j], relayed[j])
        added = more if added is None else added + more
    lanes = lax.broadcasted_iota(jnp.int32, (64, 128), 1)
    copies = []
    for f in range(4):
        step = total[f] + added[64 * f : 64 * f + 64]
        face = pltpu.roll(pltpu.roll(step[:, :128], 64, 1), 63, 0)
        tail = jnp.where(lanes < 64, step[:, 384:], face)
        step = jnp.concatenate([step[:, :384], tail], axis=1)
        ready[f] = (density[...] if f == 0 else momentum[f - 1]) + step
        target = new_density if f == 0 else new_momentum.at[f - 1]
        copies.append(pltpu.make_async_copy(ready.at[f], target, arrived.at[f]))
        copies[f].start()
    for copy in copies:
        copy.wait()


def relay_pairs(mesh_shape, step):
    groups, members = mesh_shape
    pairs = []
    for g in range(groups):
        for m in range(members):
            core = m % 2
            if step < 2:
                target = (g, m ^ (1 << (2 - step + 2 * core)))
            else:
                target = ((g + 1 - 2 * core) % groups, m)
            pairs.append((g * members + m, target[0] * members + target[1]))
    return pairs


def local(
    density, momentum, element_size, section_slots, section_counts, cross_slots, cross_counts
):
    rho, mom = density[0, 0], momentum[0, 0]
    sizes = element_size.reshape(3, 1, 64)
    slots = section_slots.shape[-1]
    section = section_slots.reshape(5, 1, slots)
    cross = cross_slots[0, 0]
    core = (lax.axis_index("cube") & 1).reshape(1)
    where = (section, cross, section_counts[0, 0], cross_counts[0, 0], core)
    whole = pl.BlockSpec(memory_space=pltpu.VMEM)
    scalars = pl.BlockSpec(memory_space=pltpu.SMEM)
    where_specs = [whole] * 2 + [scalars] * 3
    members = lax.axis_size("cube")
    groups = lax.axis_size("grp")
    near = [(i, i ^ 1) for i in range(members)]

    def on_chip(value):
        return pltpu.with_memory_space_constraint(value, pltpu.VMEM)

    def near_chip(shape, dtype=F32):
        return pltpu.VMEM(shape, dtype)

    steps, table, volumes, sent = pl.pallas_call(
        sums_kernel,
        out_shape=(
            near_chip((4, 64, 512)),
            near_chip((528, 512), BF16),
            near_chip((2, 64, 128)),
            near_chip((4, 5, 8, 128)),
        ),
        in_specs=[whole] * 7 + where_specs,
        out_specs=(whole,) * 4,
        name="sums_and_gather",
    )(rho, mom, sizes, *[jnp.asarray(t) for t in tables()], *where)

    shared = lax.ppermute(sent, "cube", near)
    own = pl.pallas_call(
        gather_kernel,
        out_shape=near_chip((3, 5, 8, 128)),
        in_specs=[whole] * 2 + where_specs,
        out_specs=whole,
        name="gather",
    )(on_chip(table), on_chip(volumes), *where)

    far = [None] * 3
    for step in range(3):
        both = jnp.stack([own[step], shared[step + 1]])
        part = lax.ppermute(both, ("grp", "cube"), relay_pairs((groups, members), step))
        far[step] = on_chip(part)
    back = pl.pallas_call(
        pack_kernel,
        out_shape=near_chip((3, 5, 8, 128)),
        in_specs=[whole] * 3,
        out_specs=whole,
        name="pack",
    )(*far)
    relayed = lax.ppermute(back, "cube", near)
    total = pl.pallas_call(
        scatter_kernel,
        out_shape=near_chip((4, 64, 512)),
        in_specs=[whole] + where_specs + [whole] * 6,
        out_specs=whole,
        name="scatter",
    )(on_chip(steps), *where, on_chip(sent), on_chip(own), on_chip(shared), *far)
    hbm = pl.BlockSpec(memory_space=pl.ANY)
    new_density, new_momentum = pl.pallas_call(
        update_kernel,
        out_shape=(
            jax.ShapeDtypeStruct(rho.shape, F32),
            jax.ShapeDtypeStruct(mom.shape, F32),
        ),
        in_specs=[whole] * 3 + where_specs + [whole] * 3,
        out_specs=(hbm, hbm),
        scratch_shapes=[pltpu.VMEM((4, 64, 512), F32), pltpu.SemaphoreType.DMA((4,))],
        name="scatter_and_update",
    )(on_chip(rho), on_chip(mom), on_chip(total), *where, on_chip(sent), on_chip(own), on_chip(relayed))
    return (new_density[None, None], new_momentum[None, None])


def solution(mesh):
    placed = (
        P("grp", "cube", None, None),
        P("grp", "cube", None, None, None),
        P("grp", "cube", None, None),
        P("grp", "cube", None, None),
        P("grp", "cube", None),
        P("grp", "cube", None, None),
        P("grp", "cube", None),
    )

    return jax.shard_map(
        local,
        mesh=mesh,
        in_specs=placed,
        out_specs=(P("grp", "cube", None, None), P("grp", "cube", None, None, None)),
        check_vma=False,
    )
```

profile of v0, /device:TPU:1, one launch (start us, length us, event | category | flops | bytes accessed | tf_op | source)
XLA Modules:
  0.0 41.8 jit_solution(13877019997193878015)
XLA Ops:
  0.6 5.4 %sums_and_gather.1 = (f32[4,64,512]{2,1,0:T(8,128)S(1)}, bf16[528,512]{1,0:T(8,128)(2,1)S(1)}, f32[2,64,128]{2,1,0:T(8,128)S(1)}, f32[4,5,8,128]{3,2,1,0:T(8,128)S(1)}) custom-call(f32[64,512]{1,0:T(8,128)} %bitcast.12, f32[3,64,512]{2,1,0:T(8,128)} %bitcast.10, f32[3,1,64]{2,1,0:T(1,128)} %bitcast.30, bf16[2,512,512]{2,1,0:T(8,128)(2,1)} %constant.14.clone.first, ...), custom_call_target="tpu_custom_call" | custom-call | tf_op jit(solution)/shard_map/sums_and_gather/pallas_call | solution.py:326
  6.1 8.7 %collective-permute-start = (f32[4,5,8,128]{3,2,1,0:T(8,128)S(1)}, f32[4,5,8,128]{3,2,1,0:T(8,128)S(1)}, u32[]{:S(2)}, u32[]{:S(2)}) collective-permute-start(f32[4,5,8,128]{3,2,1,0:T(8,128)S(1)} %get-tuple-element.9.sent), channel_id=1, source_target_pairs={{0,1},{1,0},{2,3},{3,2},{4,5},{5,4},{6,7},{7,6},{8,9},{9,8},{10,11... | collective-permute-start | bytes 245768 | tf_op jit(solution)/shard_map/ppermute | solution.py:339
  14.8 2.8 %gather.1.own = f32[3,5,8,128]{3,2,1,0:T(8,128)S(1)} custom-call(bf16[528,512]{1,0:T(8,128)(2,1)S(1)} %get-tuple-element.10.table, f32[2,64,128]{2,1,0:T(8,128)S(1)} %get-tuple-element.11.volumes, s32[5,1,1024]{2,1,0:T(1,128)} %bitcast.15, s32[2,1024]{1,0:T(2,128)} %bitcast.19, s32[5]{0:T(128)} %bitcast.23, s32[2]{0:T(128)} %bitcast.27, s32[1]{0:T(128)} %bitcast.7.core), custom_call_target="tpu_custom_call" | custom-call | tf_op jit(solution)/shard_map/gather/pallas_call | solution.py:340
  17.6 0.0 collective-permute-done.shared
  17.6 1.9 %collective-permute-start.1 = (f32[2,5,8,128]{3,2,1,0:T(8,128)S(1)}, f32[2,5,8,128]{3,2,1,0:T(8,128)S(1)}, u32[]{:S(2)}, u32[]{:S(2)}) collective-permute-start(f32[2,5,8,128]{3,2,1,0:T(8,128)S(1)} %pad_maximum_fusion), channel_id=1, source_target_pairs={{0,4},{1,17},{2,6},{3,19},{4,0},{5,21},{6,2},{7,23},{8,12},{9,25},... | collective-permute-start | bytes 122888 | tf_op jit(solution)/shard_map/ppermute | solution.py:351
  19.6 1.9 %collective-permute-start.2 = (f32[2,5,8,128]{3,2,1,0:T(8,128)S(1)}, f32[2,5,8,128]{3,2,1,0:T(8,128)S(1)}, u32[]{:S(2)}, u32[]{:S(2)}) collective-permute-start(f32[2,5,8,128]{3,2,1,0:T(8,128)S(1)} %pad_maximum_fusion.1), channel_id=1, source_target_pairs={{0,2},{1,9},{2,0},{3,11},{4,6},{5,13},{6,4},{7,15},{8,10},{9,1},{1... | collective-permute-start | bytes 122888 | tf_op jit(solution)/shard_map/ppermute | solution.py:351
  21.5 9.1 %collective-permute-start.3 = (f32[2,5,8,128]{3,2,1,0:T(8,128)S(1)}, f32[2,5,8,128]{3,2,1,0:T(8,128)S(1)}, u32[]{:S(2)}, u32[]{:S(2)}) collective-permute-start(f32[2,5,8,128]{3,2,1,0:T(8,128)S(1)} %pad_maximum_fusion.2), channel_id=1, source_target_pairs={{0,32},{1,481},{2,34},{3,483},{4,36},{5,485},{6,38},{7,487},{8,40}... | collective-permute-start | bytes 122888 | tf_op jit(solution)/shard_map/ppermute | solution.py:351
  30.6 0.0 collective-permute-done.1.far_a
  30.6 0.0 collective-permute-done.2.far_b
  30.6 1.1 %collective-permute-done.3.far_c = f32[2,5,8,128]{3,2,1,0:T(8,128)S(1)} collective-permute-done((f32[2,5,8,128]{3,2,1,0:T(8,128)S(1)}, f32[2,5,8,128]{3,2,1,0:T(8,128)S(1)}, u32[]{:S(2)}, u32[]{:S(2)}) %collective-permute-start.3) | collective-permute-done | bytes 40992 | tf_op jit(solution)/shard_map/ppermute | solution.py:351
  31.7 3.4 %collective-permute-start.4 = (f32[3,5,8,128]{3,2,1,0:T(8,128)S(1)}, f32[3,5,8,128]{3,2,1,0:T(8,128)S(1)}, u32[]{:S(2)}, u32[]{:S(2)}) collective-permute-start(f32[3,5,8,128]{3,2,1,0:T(8,128)S(1)} %pack.1), channel_id=1, source_target_pairs={{0,1},{1,0},{2,3},{3,2},{4,5},{5,4},{6,7},{7,6},{8,9},{9,8},{10,11... | collective-permute-start | bytes 184328 | tf_op jit(solution)/shard_map/ppermute | solution.py:360
  35.1 0.0 copy-start
  35.1 0.0 copy-start.1
  35.1 3.2 %scatter.1.total = f32[4,64,512]{2,1,0:T(8,128)S(1)} custom-call(f32[4,64,512]{2,1,0:T(8,128)S(1)} %get-tuple-element.8.steps, s32[5,1,1024]{2,1,0:T(1,128)} %bitcast.16, s32[2,1024]{1,0:T(2,128)} %bitcast.20, s32[5]{0:T(128)} %bitcast.24, s32[2]{0:T(128)} %bitcast.28, s32[1]{0:T(128)} %bitcast.7.core, f32[4,5,8,128]{3,2,1,0:T(8,128)S(1)} %get-tuple-element.9.sent, ...), custom_call_target="tpu_custom_call" | custom-call | tf_op jit(solution)/shard_map/scatter/pallas_call | solution.py:361
  38.3 0.0 collective-permute-done.4.relayed
  38.3 0.0 copy-done
  38.3 0.0 copy-done.1
  38.3 3.5 %scatter_and_update.1 = (f32[64,512]{1,0:T(8,128)}, f32[3,64,512]{2,1,0:T(8,128)}) custom-call(f32[64,512]{1,0:T(8,128)S(1)} %bitcast.13, f32[3,64,512]{2,1,0:T(8,128)S(1)} %bitcast.11, f32[4,64,512]{2,1,0:T(8,128)S(1)} %scatter.1.total, s32[5,1,1024]{2,1,0:T(1,128)} %bitcast.17, s32[2,1024]{1,0:T(2,128)} %bitcast.21, s32[5]{0:T(128)} %bitcast.25, ...), custom_call_target="tpu_custom_call" | custom-call | tf_op jit(solution)/shard_map/scatter_and_update/pallas_call | solution.py:369
  (6 shorter events, 0.0 us)
Async XLA Ops:
  6.1 11.6 %collective-permute-start = (f32[4,5,8,128]{3,2,1,0:T(8,128)S(1)}, f32[4,5,8,128]{3,2,1,0:T(8,128)S(1)}, u32[]{:S(2)}, u32[]{:S(2)}) collective-permute-start(f32[4,5,8,128]{3,2,1,0:T(8,128)S(1)} %get-tuple-element.9.sent), channel_id=1, source_target_pairs={{0,1},{1,0},{2,3},{3,2},{4,5},{5,4},{6,7},{7,6},{8,9},{9,8},{10,11... | collective-permute-start | bytes 245768 | tf_op jit(solution)/shard_map/ppermute | solution.py:339
  17.6 13.0 %collective-permute-start.1 = (f32[2,5,8,128]{3,2,1,0:T(8,128)S(1)}, f32[2,5,8,128]{3,2,1,0:T(8,128)S(1)}, u32[]{:S(2)}, u32[]{:S(2)}) collective-permute-start(f32[2,5,8,128]{3,2,1,0:T(8,128)S(1)} %pad_maximum_fusion), channel_id=1, source_target_pairs={{0,4},{1,17},{2,6},{3,19},{4,0},{5,21},{6,2},{7,23},{8,12},{9,25},... | collective-permute-start | bytes 122888 | tf_op jit(solution)/shard_map/ppermute | solution.py:351
  19.6 11.0 %collective-permute-start.2 = (f32[2,5,8,128]{3,2,1,0:T(8,128)S(1)}, f32[2,5,8,128]{3,2,1,0:T(8,128)S(1)}, u32[]{:S(2)}, u32[]{:S(2)}) collective-permute-start(f32[2,5,8,128]{3,2,1,0:T(8,128)S(1)} %pad_maximum_fusion.1), channel_id=1, source_target_pairs={{0,2},{1,9},{2,0},{3,11},{4,6},{5,13},{6,4},{7,15},{8,10},{9,1},{1... | collective-permute-start | bytes 122888 | tf_op jit(solution)/shard_map/ppermute | solution.py:351
  21.5 10.2 %collective-permute-start.3 = (f32[2,5,8,128]{3,2,1,0:T(8,128)S(1)}, f32[2,5,8,128]{3,2,1,0:T(8,128)S(1)}, u32[]{:S(2)}, u32[]{:S(2)}) collective-permute-start(f32[2,5,8,128]{3,2,1,0:T(8,128)S(1)} %pad_maximum_fusion.2), channel_id=1, source_target_pairs={{0,32},{1,481},{2,34},{3,483},{4,36},{5,485},{6,38},{7,487},{8,40}... | collective-permute-start | bytes 122888 | tf_op jit(solution)/shard_map/ppermute | solution.py:351
  31.7 6.6 %collective-permute-start.4 = (f32[3,5,8,128]{3,2,1,0:T(8,128)S(1)}, f32[3,5,8,128]{3,2,1,0:T(8,128)S(1)}, u32[]{:S(2)}, u32[]{:S(2)}) collective-permute-start(f32[3,5,8,128]{3,2,1,0:T(8,128)S(1)} %pack.1), channel_id=1, source_target_pairs={{0,1},{1,0},{2,3},{3,2},{4,5},{5,4},{6,7},{7,6},{8,9},{9,8},{10,11... | collective-permute-start | bytes 184328 | tf_op jit(solution)/shard_map/ppermute | solution.py:360
  35.1 3.2 %copy-start = (f32[1,1,3,64,512]{4,3,2,1,0:T(8,128)S(1)}, f32[1,1,3,64,512]{4,3,2,1,0:T(8,128)}, u32[]{:S(2)}) copy-start(f32[1,1,3,64,512]{4,3,2,1,0:T(8,128)} %param.12) | copy-start | bytes 1179652
  35.1 3.2 %copy-start.1 = (f32[1,1,64,512]{3,2,1,0:T(8,128)S(1)}, f32[1,1,64,512]{3,2,1,0:T(8,128)}, u32[]{:S(2)}) copy-start(f32[1,1,64,512]{3,2,1,0:T(8,128)} %param.11) | copy-start | bytes 393220
where the time goes:
time: 42.2 us; the launch traced here: 41.8 us
  starting transfers between devices  25 us (59%)
  Pallas kernels  14.9 us (35%)
  waiting for transfers between devices  1.07 us (3%)
  between operations  0.8 us (2%)
    ppermute x3, starting transfers between devices, local(): lax.ppermute(both, ('grp', 'cube'), relay_pairs((groups, members), step))  12.9 us
    ppermute x1, starting transfers between devices, local(): shared = lax.ppermute(sent, 'cube', near)  8.75 us
    pallas_call x1, Pallas kernels, local(): pl.pallas_call(sums_kernel, out_shape=(near_chip((4, 64, 512)), near_chip...  5.41 us
    pallas_call x1, Pallas kernels, local(): pl.pallas_call(update_kernel, out_shape=(jax.ShapeDtypeStruct(rho.shape,...  3.49 us
    ppermute x1, starting transfers between devices, local(): relayed = lax.ppermute(back, 'cube', near)  3.37 us
    pallas_call x1, Pallas kernels, local(): pl.pallas_call(scatter_kernel, out_shape=near_chip((4, 64, 512)), in_spec...  3.18 us
    pallas_call x1, Pallas kernels, local(): pl.pallas_call(gather_kernel, out_shape=near_chip((3, 5, 8, 128)), in_spe...  2.78 us
    ppermute x3, waiting for transfers between devices, local(): lax.ppermute(both, ('grp', 'cube'), relay_pairs((groups, members), step))  1.06 us
  transfers between devices with their start and end apart: 5, of which 1 were waited for; matrix products, arithmetic and copies ran while one was open for 0% of the time, Pallas kernels for 14%

commit v1 on v0

--- a/solution.py
+++ b/solution.py
@@ -69,10 +69,15 @@
 
 def tables():
     _, weights, derivative = gll_tables()
-    along_first = np.kron(derivative, np.eye(64)).T
     along_second = np.kron(np.eye(4), np.kron(derivative, np.eye(8))).T
     along_third = np.kron(np.eye(32), derivative).T
-    first = np.stack(bf16_parts(along_first, 2))
+    first = np.zeros((32, 128), np.float32)
+    for t in range(4):
+        for s in range(4):
+            for r in range(2):
+                for half in range(2):
+                    factor = derivative[2 * t + half, 2 * s + (half ^ r)]
+                    first[8 * t + 2 * s + r, 64 * half : 64 * half + 64] = factor
     inner = np.stack(bf16_parts(along_second, 2) + bf16_parts(along_third, 2))
     node = np.kron(weights, np.kron(weights, weights)).astype(np.float32)[None]
     node_parts = np.concatenate(
@@ -179,7 +184,7 @@
 
 def sums_kernel(
     density, momentum, sizes, first, inner, node, node_parts, section, cross, section_n, cross_n,
-    core, steps, table, volumes, send,
+    code, steps, table, volumes, send, far_own, near_own,
 ):
     rho = density[...]
     inverse = 1.0 / rho
@@ -195,18 +200,31 @@
         for a in range(3):
             part = mom[a] * velocity[d]
             parts.append(part + pressure if a == d else part)
-        return split(jnp.concatenate([part * scale[d] for part in parts], axis=0))
-
-    high, low = flux(0)
-    change = dot(high, first[0]) + dot(low, first[0]) + dot(high, first[1])
-    halves = [change[:, :256], change[:, 256:]]
+        return [part * scale[d] for part in parts]
+
+    def along_first(part):
+        tiles = [part[:, 128 * t : 128 * t + 128] for t in range(4)]
+        swapped = [pltpu.roll(tile, 64, 1) for tile in tiles]
+        outs = []
+        for t in range(4):
+            out = None
+            for s in range(4):
+                for r, tile in enumerate((tiles[s], swapped[s])):
+                    at = 8 * t + 2 * s + r
+                    term = tile * first[at : at + 1, :]
+                    out = term if out is None else out + term
+            outs.append(out)
+        return jnp.concatenate(outs, axis=1)
+
+    halves = [None, None]
     for d in (1, 2):
-        high, low = flux(d)
+        high, low = split(jnp.concatenate(flux(d), axis=0))
         big, small = inner[2 * d - 2], inner[2 * d - 1]
         for k in range(2):
             lanes = slice(256 * k, 256 * k + 256)
-            halves[k] += dot(high[:, lanes], big) + dot(low[:, lanes], big)
-            halves[k] += dot(high[:, lanes], small)
+            half = dot(high[:, lanes], big) + dot(low[:, lanes], big) + dot(high[:, lanes], small)
+            halves[k] = half if halves[k] is None else halves[k] + half
+    fluxes = flux(0)
     change = jnp.concatenate(halves, axis=1)
     node_w = node[...]
 
@@ -217,7 +235,7 @@
 
     share = DT / with_face(jacobian * node_w)
     for f in range(4):
-        value = with_face(-change[64 * f : 64 * f + 64] * node_w)
+        value = with_face(-(change[64 * f : 64 * f + 64] + along_first(fluxes[f])) * node_w)
         steps[f] = value * share
         high, low = split(value)
         table[64 * f : 64 * f + 64, :] = high
@@ -226,51 +244,72 @@
     volumes[0] = jnp.broadcast_to(jacobian, (64, 128))
     volumes[1] = pltpu.roll(volumes[0], 1, 0)
 
-    pick(table, volumes, section[0], section_n[0], send, 0)
-    ids = carried(1 - core[0], section, cross, False)
-    counts = carried_counts(1 - core[0], section_n, cross_n, False)
-    for j in range(3):
-        pick(table, volumes, ids[j], counts[j], send, j + 1)
-
-
-def gather_kernel(table, volumes, section, cross, section_n, cross_n, core, send):
-    ids = carried(core[0], section, cross, False)
-    counts = carried_counts(core[0], section_n, cross_n, False)
+    side = code[0] & 1
+    ids = carried(1 - side, section, cross, False)
+    counts = carried_counts(1 - side, section_n, cross_n, False)
     for j in range(3):
         pick(table, volumes, ids[j], counts[j], send, j)
 
-
-def pack_kernel(far_a, far_b, far_c, back):
+    @pl.when(code[0] >= 2)
+    def _():
+        pick_far(table, volumes, section, cross, section_n, cross_n, side, far_own)
+        pick_near(table, volumes, section, section_n, side, near_own)
+
+
+def pick_far(table, volumes, section, cross, section_n, cross_n, side, own):
+    ids = carried(side, section, cross, False)[2]
+    pick(table, volumes, ids, carried_counts(side, section_n, cross_n, False)[2], own, 0)
+
+
+def pick_near(table, volumes, section, section_n, side, own):
+    for j, at in enumerate((2 + 2 * side, 1 + 2 * side, 0)):
+        pick(table, volumes, section[at], section_n[at], own, j)
+
+
+def far_kernel(table, volumes, section, cross, section_n, cross_n, code, before, own):
+    @pl.when(code[0] < 2)
+    def _():
+        pick_far(table, volumes, section, cross, section_n, cross_n, code[0] & 1, own)
+
+
+def near_kernel(table, volumes, section, cross, section_n, cross_n, code, before, own):
+    @pl.when(code[0] < 2)
+    def _():
+        pick_near(table, volumes, section, section_n, code[0] & 1, own)
+
+
+def pack_kernel(far_a, far_b, far_c, own, back):
     for j, far in enumerate((far_a, far_b, far_c)):
         back[j] = far[1]
+    back[3] = own[2]
 
 
 def scatter_kernel(
-    steps, section, cross, section_n, cross_n, core, sent, own, shared, far_a, far_b, far_c, total
+    steps, section, cross, section_n, cross_n, code, sent, near_own, far_a, far_b, far_c, total
 ):
-    side = core[0]
+    side = code[0] & 1
     ids = carried(side, section, cross, True)
     counts = carried_counts(side, section_n, cross_n, True)
-    added = spread(section[0], section_n[0], sent[0], shared[0])
-    mine = (own[0], own[1], sent[3])
+    mine = (near_own[0], near_own[1], sent[2])
+    added = None
     for j, far in enumerate((far_a, far_b, far_c)):
-        added += spread(ids[j], counts[j], mine[j], far[0])
+        more = spread(ids[j], counts[j], mine[j], far[0])
+        added = more if added is None else added + more
     for f in range(4):
         total[f] = steps[f] + added[64 * f : 64 * f + 64]
 
 
 def update_kernel(
-    density, momentum, total, section, cross, section_n, cross_n, core, sent, own, relayed,
-    new_density, new_momentum, ready, arrived,
+    density, momentum, total, section, cross, section_n, cross_n, code, sent, near_own, far_own,
+    relayed, new_density, new_momentum, ready, arrived,
 ):
-    side = 1 - core[0]
+    side = 1 - (code[0] & 1)
     ids = carried(side, section, cross, True)
     counts = carried_counts(side, section_n, cross_n, True)
-    mine = (sent[1], sent[2], own[2])
-    added = None
+    mine = (sent[0], sent[1], far_own[0])
+    added = spread(section[0], section_n[0], near_own[2], relayed[3])
     for j in range(3):
-        more = spread(ids[j], counts[j], mine[j], relayed[j])
-        added = more if added is None else added + more
+        added += spread(ids[j], counts[j], mine[j], relayed[j])
     lanes = lax.broadcasted_iota(jnp.int32, (64, 128), 1)
     copies = []
     for f in range(4):
@@ -308,13 +347,15 @@
     slots = section_slots.shape[-1]
     section = section_slots.reshape(5, 1, slots)
     cross = cross_slots[0, 0]
-    core = (lax.axis_index("cube") & 1).reshape(1)
-    where = (section, cross, section_counts[0, 0], cross_counts[0, 0], core)
+    members = lax.axis_size("cube")
+    groups = lax.axis_size("grp")
+    device = lax.axis_index("grp") * members + lax.axis_index("cube")
+    early = jnp.logical_and(device > 0, device < members)
+    code = ((device & 1) + 2 * early.astype(jnp.int32)).reshape(1)
+    where = (section, cross, section_counts[0, 0], cross_counts[0, 0], code)
     whole = pl.BlockSpec(memory_space=pltpu.VMEM)
     scalars = pl.BlockSpec(memory_space=pltpu.SMEM)
     where_specs = [whole] * 2 + [scalars] * 3
-    members = lax.axis_size("cube")
-    groups = lax.axis_size("grp")
     near = [(i, i ^ 1) for i in range(members)]
 
     def on_chip(value):
@@ -323,48 +364,55 @@
     def near_chip(shape, dtype=F32):
         return pltpu.VMEM(shape, dtype)
 
-    steps, table, volumes, sent = pl.pallas_call(
+    section_sums = (5, 8, 128)
+    steps, table, volumes, sent, far_own, near_own = pl.pallas_call(
         sums_kernel,
         out_shape=(
             near_chip((4, 64, 512)),
             near_chip((528, 512), BF16),
             near_chip((2, 64, 128)),
-            near_chip((4, 5, 8, 128)),
+            near_chip((3,) + section_sums),
+            near_chip((1,) + section_sums),
+            near_chip((3,) + section_sums),
         ),
         in_specs=[whole] * 7 + where_specs,
-        out_specs=(whole,) * 4,
+        out_specs=(whole,) * 6,
         name="sums_and_gather",
     )(rho, mom, sizes, *[jnp.asarray(t) for t in tables()], *where)
-
     shared = lax.ppermute(sent, "cube", near)
-    own = pl.pallas_call(
-        gather_kernel,
-        out_shape=near_chip((3, 5, 8, 128)),
-        in_specs=[whole] * 2 + where_specs,
-        out_specs=whole,
-        name="gather",
-    )(on_chip(table), on_chip(volumes), *where)
-
+
+    def gather(kernel, own):
+        return pl.pallas_call(
+            kernel,
+            out_shape=near_chip(own.shape),
+            in_specs=[whole] * 2 + where_specs + [whole],
+            out_specs=whole,
+            input_output_aliases={7: 0},
+        )(on_chip(table), on_chip(volumes), *where, on_chip(own))
+
+    far_own = gather(far_kernel, far_own)
+    near_own = gather(near_kernel, near_own)
     far = [None] * 3
     for step in range(3):
-        both = jnp.stack([own[step], shared[step + 1]])
+        own = far_own[0] if step == 2 else near_own[step]
+        both = jnp.stack([own, shared[step]])
         part = lax.ppermute(both, ("grp", "cube"), relay_pairs((groups, members), step))
         far[step] = on_chip(part)
     back = pl.pallas_call(
         pack_kernel,
-        out_shape=near_chip((3, 5, 8, 128)),
-        in_specs=[whole] * 3,
+        out_shape=near_chip((4,) + section_sums),
+        in_specs=[whole] * 4,
         out_specs=whole,
         name="pack",
-    )(*far)
+    )(*far, on_chip(near_own))
     relayed = lax.ppermute(back, "cube", near)
     total = pl.pallas_call(
         scatter_kernel,
         out_shape=near_chip((4, 64, 512)),
-        in_specs=[whole] + where_specs + [whole] * 6,
+        in_specs=[whole] + where_specs + [whole] * 5,
         out_specs=whole,
         name="scatter",
-    )(on_chip(steps), *where, on_chip(sent), on_chip(own), on_chip(shared), *far)
+    )(on_chip(steps), *where, on_chip(sent), on_chip(near_own), *far)
     hbm = pl.BlockSpec(memory_space=pl.ANY)
     new_density, new_momentum = pl.pallas_call(
         update_kernel,
@@ -372,11 +420,14 @@
             jax.ShapeDtypeStruct(rho.shape, F32),
             jax.ShapeDtypeStruct(mom.shape, F32),
         ),
-        in_specs=[whole] * 3 + where_specs + [whole] * 3,
+        in_specs=[whole] * 3 + where_specs + [whole] * 4,
         out_specs=(hbm, hbm),
         scratch_shapes=[pltpu.VMEM((4, 64, 512), F32), pltpu.SemaphoreType.DMA((4,))],
         name="scatter_and_update",
-    )(on_chip(rho), on_chip(mom), on_chip(total), *where, on_chip(sent), on_chip(own), on_chip(relayed))
+    )(
+        on_chip(rho), on_chip(mom), on_chip(total), *where, on_chip(sent), on_chip(near_own),
+        on_chip(far_own), on_chip(relayed),
+    )
     return (new_density[None, None], new_momentum[None, None])
 
 

time: 42.2 us -> 42.7 us (1.012)
    ppermute x3, starting transfers between devices: 12.9 us -> 15.7 us  [local(): lax.ppermute(both, ('grp', 'cube'), relay_pairs((groups, members), step))]
    ppermute x1, starting transfers between devices: 8.75 us -> 6.13 us  [local(): shared = lax.ppermute(sent, 'cube', near)]
    pallas_call x1, Pallas kernels: 5.41 us -> 6.88 us  [local(): pl.pallas_call(sums_kernel, out_shape=(near_chip((4, 64, 512)), near_chip...]
    pallas_call x2 -> x3, Pallas kernels: 2.79 us -> 1.65 us  [the longest x2 1.64 us: gather(): pl.pallas_call(kernel, out_shape=near_chip(own.shape), in_specs=[whole] *...]
    pallas_call x1, Pallas kernels: 3.18 us -> 2.64 us  [local(): pl.pallas_call(scatter_kernel, out_shape=near_chip((4, 64, 512)), in_spec...]
    pallas_call x1, Pallas kernels: 3.49 us -> 4.02 us  [local(): pl.pallas_call(update_kernel, out_shape=(jax.ShapeDtypeStruct(rho.shape,...]
  transfers between devices with their start and end apart: 5 -> 5, of which waited for: 1 -> 1; matrix products, arithmetic and copies ran while one was open for 0% -> 0% of each run, Pallas kernels for 14% -> 10%
where the time goes in v1:
time: 42.7 us; the launch traced here: 42.3 us
  starting transfers between devices  25.2 us (59%)
  Pallas kernels  15.2 us (36%)
  waiting for transfers between devices  1.07 us (3%)
  between operations  0.82 us (2%)
    ppermute x3, starting transfers between devices, local(): lax.ppermute(both, ('grp', 'cube'), relay_pairs((groups, members), step))  15.7 us
    pallas_call x1, Pallas kernels, local(): pl.pallas_call(sums_kernel, out_shape=(near_chip((4, 64, 512)), near_chip...  6.88 us
    ppermute x1, starting transfers between devices, local(): shared = lax.ppermute(sent, 'cube', near)  6.13 us
    pallas_call x1, Pallas kernels, local(): pl.pallas_call(update_kernel, out_shape=(jax.ShapeDtypeStruct(rho.shape,...  4.02 us
    ppermute x1, starting transfers between devices, local(): relayed = lax.ppermute(back, 'cube', near)  3.38 us
    pallas_call x1, Pallas kernels, local(): pl.pallas_call(scatter_kernel, out_shape=near_chip((4, 64, 512)), in_spec...  2.64 us
    pallas_call x2, Pallas kernels, gather(): pl.pallas_call(kernel, out_shape=near_chip(own.shape), in_specs=[whole] *...  1.64 us
    ppermute x3, waiting for transfers between devices, local(): lax.ppermute(both, ('grp', 'cube'), relay_pairs((groups, members), step))  1.06 us
  transfers between devices with their start and end apart: 5, of which 1 were waited for; matrix products, arithmetic and copies ran while one was open for 0% of the time, Pallas kernels for 10%

profile of v1, /device:TPU:1, one launch (start us, length us, event | category | flops | bytes accessed | tf_op | source)
XLA Modules:
  0.0 42.3 jit_solution(11638764335208905517)
XLA Ops:
  0.6 6.9 %sums_and_gather.1 = (f32[4,64,512]{2,1,0:T(8,128)S(1)}, bf16[528,512]{1,0:T(8,128)(2,1)S(1)}, f32[2,64,128]{2,1,0:T(8,128)S(1)}, f32[3,5,8,128]{3,2,1,0:T(8,128...) custom-call(f32[64,512]{1,0:T(8,128)} %bitcast.12, f32[3,64,512]{2,1,0:T(8,128)} %bitcast.10, ...), custom_call_target="tpu_custom_call" | custom-call | tf_op jit(solution)/shard_map/sums_and_gather/pallas_call | solution.py:368
  7.5 6.1 %collective-permute-start = (f32[3,5,8,128]{3,2,1,0:T(8,128)S(1)}, f32[3,5,8,128]{3,2,1,0:T(8,128)S(1)}, u32[]{:S(2)}, u32[]{:S(2)}) collective-permute-start(f32[3,5,8,128]{3,2,1,0:T(8,128)S(1)} %get-tuple-element.11.sent), channel_id=1, source_target_pairs={{0,1},{1,0},{2,3},{3,2},{4,5},{5,4},{6,7},{7,6},{8,9},{9,8},{10,11... | collective-permute-start | bytes 184328 | tf_op jit(solution)/shard_map/ppermute | solution.py:382
  13.7 0.8 %shard_map.122.near_own.own = f32[3,5,8,128]{3,2,1,0:T(8,128)S(1)} custom-call(bf16[528,512]{1,0:T(8,128)(2,1)S(1)} %get-tuple-element.12.table, f32[2,64,128]{2,1,0:T(8,128)S(1)} %get-tuple-element.13.volumes, s32[5,1,1024]{2,1,0:T(1,128)} %bitcast.15, s32[2,1024]{1,0:T(2,128)} %bitcast.20, s32[5]{0:T(128)} %bitcast.25, ...), custom_call_target="tpu_custom_call", output_to_operand_aliasing={{}: (7, {})} | custom-call | tf_op jit(solution)/shard_map/pallas_call | solution.py:385
  14.5 0.8 %shard_map.123.far_own = f32[1,5,8,128]{3,2,1,0:T(8,128)S(1)} custom-call(bf16[528,512]{1,0:T(8,128)(2,1)S(1)} %get-tuple-element.12.table, f32[2,64,128]{2,1,0:T(8,128)S(1)} %get-tuple-element.13.volumes, s32[5,1,1024]{2,1,0:T(1,128)} %bitcast.16, s32[2,1024]{1,0:T(2,128)} %bitcast.21, s32[5]{0:T(128)} %bitcast.26, ...), custom_call_target="tpu_custom_call", output_to_operand_aliasing={{}: (7, {})} | custom-call | tf_op jit(solution)/shard_map/pallas_call | solution.py:385
  15.3 0.0 collective-permute-done
  15.4 2.1 %collective-permute-start.1 = (f32[2,5,8,128]{3,2,1,0:T(8,128)S(1)}, f32[2,5,8,128]{3,2,1,0:T(8,128)S(1)}, u32[]{:S(2)}, u32[]{:S(2)}) collective-permute-start(f32[2,5,8,128]{3,2,1,0:T(8,128)S(1)} %pad_maximum_fusion), channel_id=1, source_target_pairs={{0,4},{1,17},{2,6},{3,19},{4,0},{5,21},{6,2},{7,23},{8,12},{9,25},... | collective-permute-start | bytes 122888 | tf_op jit(solution)/shard_map/ppermute | solution.py:399
  17.5 2.3 %collective-permute-start.2 = (f32[2,5,8,128]{3,2,1,0:T(8,128)S(1)}, f32[2,5,8,128]{3,2,1,0:T(8,128)S(1)}, u32[]{:S(2)}, u32[]{:S(2)}) collective-permute-start(f32[2,5,8,128]{3,2,1,0:T(8,128)S(1)} %pad_maximum_fusion.1), channel_id=1, source_target_pairs={{0,2},{1,9},{2,0},{3,11},{4,6},{5,13},{6,4},{7,15},{8,10},{9,1},{1... | collective-permute-start | bytes 122888 | tf_op jit(solution)/shard_map/ppermute | solution.py:399
  19.8 11.3 %collective-permute-start.3 = (f32[2,5,8,128]{3,2,1,0:T(8,128)S(1)}, f32[2,5,8,128]{3,2,1,0:T(8,128)S(1)}, u32[]{:S(2)}, u32[]{:S(2)}) collective-permute-start(f32[2,5,8,128]{3,2,1,0:T(8,128)S(1)} %pad_maximum_fusion.2), channel_id=1, source_target_pairs={{0,32},{1,481},{2,34},{3,483},{4,36},{5,485},{6,38},{7,487},{8,40}... | collective-permute-start | bytes 122888 | tf_op jit(solution)/shard_map/ppermute | solution.py:399
  31.1 0.0 collective-permute-done.1.far_a
  31.1 0.0 collective-permute-done.2.far_b
  31.1 1.1 %collective-permute-done.3.far_c = f32[2,5,8,128]{3,2,1,0:T(8,128)S(1)} collective-permute-done((f32[2,5,8,128]{3,2,1,0:T(8,128)S(1)}, f32[2,5,8,128]{3,2,1,0:T(8,128)S(1)}, u32[]{:S(2)}, u32[]{:S(2)}) %collective-permute-start.3) | collective-permute-done | bytes 40992 | tf_op jit(solution)/shard_map/ppermute | solution.py:399
  32.2 3.4 %collective-permute-start.4 = (f32[4,5,8,128]{3,2,1,0:T(8,128)S(1)}, f32[4,5,8,128]{3,2,1,0:T(8,128)S(1)}, u32[]{:S(2)}, u32[]{:S(2)}) collective-permute-start(f32[4,5,8,128]{3,2,1,0:T(8,128)S(1)} %pack.1), channel_id=1, source_target_pairs={{0,1},{1,0},{2,3},{3,2},{4,5},{5,4},{6,7},{7,6},{8,9},{9,8},{10,11... | collective-permute-start | bytes 245768 | tf_op jit(solution)/shard_map/ppermute | solution.py:408
  35.6 0.0 copy-start
  35.6 0.0 copy-start.1
  35.6 2.6 %scatter.1.total = f32[4,64,512]{2,1,0:T(8,128)S(1)} custom-call(f32[4,64,512]{2,1,0:T(8,128)S(1)} %get-tuple-element.10.steps, s32[5,1,1024]{2,1,0:T(1,128)} %bitcast.17, s32[2,1024]{1,0:T(2,128)} %bitcast.22, s32[5]{0:T(128)} %bitcast.27, s32[2]{0:T(128)} %bitcast.32, s32[1]{0:T(128)} %bitcast.7.code, f32[3,5,8,128]{3,2,1,0:T(8,128)S(1)} %get-tuple-element.11.sent, ...), custom_call_target="tpu_custom_call" | custom-call | tf_op jit(solution)/shard_map/scatter/pallas_call | solution.py:409
  38.2 0.0 collective-permute-done.4.relayed
  38.3 0.0 copy-done
  38.3 0.0 copy-done.1
  38.3 4.0 %scatter_and_update.1 = (f32[64,512]{1,0:T(8,128)}, f32[3,64,512]{2,1,0:T(8,128)}) custom-call(f32[64,512]{1,0:T(8,128)S(1)} %bitcast.13, f32[3,64,512]{2,1,0:T(8,128)S(1)} %bitcast.11, f32[4,64,512]{2,1,0:T(8,128)S(1)} %scatter.1.total, s32[5,1,1024]{2,1,0:T(1,128)} %bitcast.18, s32[2,1024]{1,0:T(2,128)} %bitcast.23, s32[5]{0:T(128)} %bitcast.28, ...), custom_call_target="tpu_custom_call" | custom-call | tf_op jit(solution)/shard_map/scatter_and_update/pallas_call | solution.py:417
  (6 shorter events, 0.0 us)
Async XLA Ops:
  7.5 7.8 %collective-permute-start = (f32[3,5,8,128]{3,2,1,0:T(8,128)S(1)}, f32[3,5,8,128]{3,2,1,0:T(8,128)S(1)}, u32[]{:S(2)}, u32[]{:S(2)}) collective-permute-start(f32[3,5,8,128]{3,2,1,0:T(8,128)S(1)} %get-tuple-element.11.sent), channel_id=1, source_target_pairs={{0,1},{1,0},{2,3},{3,2},{4,5},{5,4},{6,7},{7,6},{8,9},{9,8},{10,11... | collective-permute-start | bytes 184328 | tf_op jit(solution)/shard_map/ppermute | solution.py:382
  15.4 15.7 %collective-permute-start.1 = (f32[2,5,8,128]{3,2,1,0:T(8,128)S(1)}, f32[2,5,8,128]{3,2,1,0:T(8,128)S(1)}, u32[]{:S(2)}, u32[]{:S(2)}) collective-permute-start(f32[2,5,8,128]{3,2,1,0:T(8,128)S(1)} %pad_maximum_fusion), channel_id=1, source_target_pairs={{0,4},{1,17},{2,6},{3,19},{4,0},{5,21},{6,2},{7,23},{8,12},{9,25},... | collective-permute-start | bytes 122888 | tf_op jit(solution)/shard_map/ppermute | solution.py:399
  17.5 13.6 %collective-permute-start.2 = (f32[2,5,8,128]{3,2,1,0:T(8,128)S(1)}, f32[2,5,8,128]{3,2,1,0:T(8,128)S(1)}, u32[]{:S(2)}, u32[]{:S(2)}) collective-permute-start(f32[2,5,8,128]{3,2,1,0:T(8,128)S(1)} %pad_maximum_fusion.1), channel_id=1, source_target_pairs={{0,2},{1,9},{2,0},{3,11},{4,6},{5,13},{6,4},{7,15},{8,10},{9,1},{1... | collective-permute-start | bytes 122888 | tf_op jit(solution)/shard_map/ppermute | solution.py:399
  19.8 12.4 %collective-permute-start.3 = (f32[2,5,8,128]{3,2,1,0:T(8,128)S(1)}, f32[2,5,8,128]{3,2,1,0:T(8,128)S(1)}, u32[]{:S(2)}, u32[]{:S(2)}) collective-permute-start(f32[2,5,8,128]{3,2,1,0:T(8,128)S(1)} %pad_maximum_fusion.2), channel_id=1, source_target_pairs={{0,32},{1,481},{2,34},{3,483},{4,36},{5,485},{6,38},{7,487},{8,40}... | collective-permute-start | bytes 122888 | tf_op jit(solution)/shard_map/ppermute | solution.py:399
  32.2 6.1 %collective-permute-start.4 = (f32[4,5,8,128]{3,2,1,0:T(8,128)S(1)}, f32[4,5,8,128]{3,2,1,0:T(8,128)S(1)}, u32[]{:S(2)}, u32[]{:S(2)}) collective-permute-start(f32[4,5,8,128]{3,2,1,0:T(8,128)S(1)} %pack.1), channel_id=1, source_target_pairs={{0,1},{1,0},{2,3},{3,2},{4,5},{5,4},{6,7},{7,6},{8,9},{9,8},{10,11... | collective-permute-start | bytes 245768 | tf_op jit(solution)/shard_map/ppermute | solution.py:408
  35.6 2.7 %copy-start = (f32[1,1,3,64,512]{4,3,2,1,0:T(8,128)S(1)}, f32[1,1,3,64,512]{4,3,2,1,0:T(8,128)}, u32[]{:S(2)}) copy-start(f32[1,1,3,64,512]{4,3,2,1,0:T(8,128)} %param.12) | copy-start | bytes 1179652
  35.6 2.7 %copy-start.1 = (f32[1,1,64,512]{3,2,1,0:T(8,128)S(1)}, f32[1,1,64,512]{3,2,1,0:T(8,128)}, u32[]{:S(2)}) copy-start(f32[1,1,64,512]{3,2,1,0:T(8,128)} %param.11) | copy-start | bytes 393220

commit v2 on v1

--- a/solution.py
+++ b/solution.py
@@ -1,3 +1,5 @@
+import functools
+
 import jax
 import jax.numpy as jnp
 import numpy as np
@@ -125,7 +127,8 @@
     element, column = element_and_column(ids)
     picked = dot(table[...], column_onehot(column))
     mask = element_mask(element)
-    live = lax.broadcasted_iota(jnp.int32, ids.shape, 1) < count
+    limit = jnp.concatenate([count[:1, :]] * 8, axis=1)
+    live = lax.broadcasted_iota(jnp.int32, ids.shape, 1) < limit
     volume = jnp.where(mask, volumes[0, :, :1], 0.0)
     face_volume = jnp.where(jnp.logical_and(mask, column < 64), volumes[1, :, :1], 0.0)
     volume = jnp.sum(volume + face_volume, axis=0, keepdims=True)
@@ -164,27 +167,32 @@
     return added[:256] + added[256:]
 
 
-def carried(side, section, cross, arriving):
-    lower = side == (0 if arriving else 1)
-    return [
-        section[2 + 2 * side],
-        section[1 + 2 * side],
-        jnp.where(lower, cross[0:1, :], cross[1:2, :]),
-    ]
-
-
-def carried_counts(side, section_n, cross_n, arriving):
-    lower = side == (0 if arriving else 1)
-    return [
-        section_n[2 + 2 * side],
-        section_n[1 + 2 * side],
-        jnp.where(lower, cross_n[0], cross_n[1]),
-    ]
+NEAR = (0, 1, 3)
+FAR = 2
+OTHERS = (4, 5, 6)
+ARRIVING = (0, 1, 6)
+RELAYED = (4, 5, 2, 3)
+
+
+def make_plan(section, cross, section_n, cross_n, code, ids, counts):
+    side = code[0] & 1
+    for row, core in ((0, side), (4, 1 - side)):
+        for j in range(2):
+            at = 2 - j + 2 * core
+            ids[row + j] = section[at]
+            counts[row + j] = jnp.full((8, 128), section_n[at], jnp.int32)
+        upper = core == 0
+        ids[row + 2 if row == 4 else FAR] = jnp.where(upper, cross[1:2, :], cross[0:1, :])
+        limit = jnp.where(upper, cross_n[1], cross_n[0])
+        counts[row + 2 if row == 4 else FAR] = jnp.full((8, 128), limit, jnp.int32)
+    ids[3] = section[0]
+    counts[3] = jnp.full((8, 128), section_n[0], jnp.int32)
+    counts[7] = jnp.full((8, 128), code[0], jnp.int32)
 
 
 def sums_kernel(
     density, momentum, sizes, first, inner, node, node_parts, section, cross, section_n, cross_n,
-    code, steps, table, volumes, send, far_own, near_own,
+    code, steps, table, volumes, send, far_own, near_own, ids, counts,
 ):
     rho = density[...]
     inverse = 1.0 / rho
@@ -244,38 +252,22 @@
     volumes[0] = jnp.broadcast_to(jacobian, (64, 128))
     volumes[1] = pltpu.roll(volumes[0], 1, 0)
 
-    side = code[0] & 1
-    ids = carried(1 - side, section, cross, False)
-    counts = carried_counts(1 - side, section_n, cross_n, False)
-    for j in range(3):
-        pick(table, volumes, ids[j], counts[j], send, j)
+    make_plan(section, cross, section_n, cross_n, code, ids, counts)
+    for j, row in enumerate(OTHERS):
+        pick(table, volumes, ids[row], counts[row], send, j)
 
     @pl.when(code[0] >= 2)
     def _():
-        pick_far(table, volumes, section, cross, section_n, cross_n, side, far_own)
-        pick_near(table, volumes, section, section_n, side, near_own)
-
-
-def pick_far(table, volumes, section, cross, section_n, cross_n, side, own):
-    ids = carried(side, section, cross, False)[2]
-    pick(table, volumes, ids, carried_counts(side, section_n, cross_n, False)[2], own, 0)
-
-
-def pick_near(table, volumes, section, section_n, side, own):
-    for j, at in enumerate((2 + 2 * side, 1 + 2 * side, 0)):
-        pick(table, volumes, section[at], section_n[at], own, j)
-
-
-def far_kernel(table, volumes, section, cross, section_n, cross_n, code, before, own):
-    @pl.when(code[0] < 2)
+        pick(table, volumes, ids[FAR], counts[FAR], far_own, 0)
+        for j, row in enumerate(NEAR):
+            pick(table, volumes, ids[row], counts[row], near_own, j)
+
+
+def late_kernel(rows, table, volumes, ids, counts, before, own):
+    @pl.when(jnp.max(counts[7]) < 2)
     def _():
-        pick_far(table, volumes, section, cross, section_n, cross_n, code[0] & 1, own)
-
-
-def near_kernel(table, volumes, section, cross, section_n, cross_n, code, before, own):
-    @pl.when(code[0] < 2)
-    def _():
-        pick_near(table, volumes, section, section_n, code[0] & 1, own)
+        for j, row in enumerate(rows):
+            pick(table, volumes, ids[row], counts[row], own, j)
 
 
 def pack_kernel(far_a, far_b, far_c, own, back):
@@ -284,32 +276,22 @@
     back[3] = own[2]
 
 
-def scatter_kernel(
-    steps, section, cross, section_n, cross_n, code, sent, near_own, far_a, far_b, far_c, total
-):
-    side = code[0] & 1
-    ids = carried(side, section, cross, True)
-    counts = carried_counts(side, section_n, cross_n, True)
-    mine = (near_own[0], near_own[1], sent[2])
-    added = None
-    for j, far in enumerate((far_a, far_b, far_c)):
-        more = spread(ids[j], counts[j], mine[j], far[0])
-        added = more if added is None else added + more
+def scatter_kernel(way, steps, ids, counts, mine, far, total):
+    row = ARRIVING[way]
+    added = spread(ids[row], counts[row], mine[way], far[0])
     for f in range(4):
         total[f] = steps[f] + added[64 * f : 64 * f + 64]
 
 
 def update_kernel(
-    density, momentum, total, section, cross, section_n, cross_n, code, sent, near_own, far_own,
-    relayed, new_density, new_momentum, ready, arrived,
+    density, momentum, total, ids, counts, sent, near_own, far_own, relayed, new_density,
+    new_momentum, ready, arrived,
 ):
-    side = 1 - (code[0] & 1)
-    ids = carried(side, section, cross, True)
-    counts = carried_counts(side, section_n, cross_n, True)
-    mine = (sent[0], sent[1], far_own[0])
-    added = spread(section[0], section_n[0], near_own[2], relayed[3])
-    for j in range(3):
-        added += spread(ids[j], counts[j], mine[j], relayed[j])
+    mine = (sent[0], sent[1], far_own[0], near_own[2])
+    added = None
+    for j, row in enumerate(RELAYED):
+        more = spread(ids[row], counts[row], mine[j], relayed[j])
+        added = more if added is None else added + more
     lanes = lax.broadcasted_iota(jnp.int32, (64, 128), 1)
     copies = []
     for f in range(4):
@@ -352,10 +334,8 @@
     device = lax.axis_index("grp") * members + lax.axis_index("cube")
     early = jnp.logical_and(device > 0, device < members)
     code = ((device & 1) + 2 * early.astype(jnp.int32)).reshape(1)
-    where = (section, cross, section_counts[0, 0], cross_counts[0, 0], code)
     whole = pl.BlockSpec(memory_space=pltpu.VMEM)
     scalars = pl.BlockSpec(memory_space=pltpu.SMEM)
-    where_specs = [whole] * 2 + [scalars] * 3
     near = [(i, i ^ 1) for i in range(members)]
 
     def on_chip(value):
@@ -365,7 +345,7 @@
         return pltpu.VMEM(shape, dtype)
 
     section_sums = (5, 8, 128)
-    steps, table, volumes, sent, far_own, near_own = pl.pallas_call(
+    steps, table, volumes, sent, far_own, near_own, ids, counts = pl.pallas_call(
         sums_kernel,
         out_shape=(
             near_chip((4, 64, 512)),
@@ -374,24 +354,30 @@
             near_chip((3,) + section_sums),
             near_chip((1,) + section_sums),
             near_chip((3,) + section_sums),
+            near_chip((7, 1, slots), jnp.int32),
+            near_chip((8, 8, 128), jnp.int32),
         ),
-        in_specs=[whole] * 7 + where_specs,
-        out_specs=(whole,) * 6,
+        in_specs=[whole] * 9 + [scalars] * 3,
+        out_specs=(whole,) * 8,
         name="sums_and_gather",
-    )(rho, mom, sizes, *[jnp.asarray(t) for t in tables()], *where)
+    )(
+        rho, mom, sizes, *[jnp.asarray(t) for t in tables()], section, cross,
+        section_counts[0, 0], cross_counts[0, 0], code,
+    )
+    plan = (on_chip(ids), on_chip(counts))
     shared = lax.ppermute(sent, "cube", near)
 
-    def gather(kernel, own):
+    def gather(rows, own):
         return pl.pallas_call(
-            kernel,
+            functools.partial(late_kernel, rows),
             out_shape=near_chip(own.shape),
-            in_specs=[whole] * 2 + where_specs + [whole],
+            in_specs=[whole] * 5,
             out_specs=whole,
-            input_output_aliases={7: 0},
-        )(on_chip(table), on_chip(volumes), *where, on_chip(own))
-
-    far_own = gather(far_kernel, far_own)
-    near_own = gather(near_kernel, near_own)
+            input_output_aliases={4: 0},
+        )(on_chip(table), on_chip(volumes), *plan, on_chip(own))
+
+    far_own = gather((FAR,), far_own)
+    near_own = gather(NEAR, near_own)
     far = [None] * 3
     for step in range(3):
         own = far_own[0] if step == 2 else near_own[step]
@@ -406,13 +392,15 @@
         name="pack",
     )(*far, on_chip(near_own))
     relayed = lax.ppermute(back, "cube", near)
-    total = pl.pallas_call(
-        scatter_kernel,
-        out_shape=near_chip((4, 64, 512)),
-        in_specs=[whole] + where_specs + [whole] * 5,
-        out_specs=whole,
-        name="scatter",
-    )(on_chip(steps), *where, on_chip(sent), on_chip(near_own), *far)
+    total = steps
+    for way in (2, 0, 1):
+        total = pl.pallas_call(
+            functools.partial(scatter_kernel, way),
+            out_shape=near_chip((4, 64, 512)),
+            in_specs=[whole] * 5,
+            out_specs=whole,
+            input_output_aliases={0: 0},
+        )(on_chip(total), *plan, on_chip(sent if way == 2 else near_own), far[way])
     hbm = pl.BlockSpec(memory_space=pl.ANY)
     new_density, new_momentum = pl.pallas_call(
         update_kernel,
@@ -420,12 +408,12 @@
             jax.ShapeDtypeStruct(rho.shape, F32),
             jax.ShapeDtypeStruct(mom.shape, F32),
         ),
-        in_specs=[whole] * 3 + where_specs + [whole] * 4,
+        in_specs=[whole] * 9,
         out_specs=(hbm, hbm),
         scratch_shapes=[pltpu.VMEM((4, 64, 512), F32), pltpu.SemaphoreType.DMA((4,))],
         name="scatter_and_update",
     )(
-        on_chip(rho), on_chip(mom), on_chip(total), *where, on_chip(sent), on_chip(near_own),
+        on_chip(rho), on_chip(mom), on_chip(total), *plan, on_chip(sent), on_chip(near_own),
         on_chip(far_own), on_chip(relayed),
     )
     return (new_density[None, None], new_momentum[None, None])

time: 42.7 us -> 40.3 us (0.944)
  Pallas kernels: 15.2 us -> 12.8 us
  starting transfers between devices: 25.2 us -> 23.3 us
  waiting for transfers between devices: 1.07 us -> 2.86 us
    pallas_call x3 -> x5, Pallas kernels: 4.28 us -> 2.72 us  [the longest x3 2.31 us: local(): pl.pallas_call(functools.partial(scatter_kernel, way), out_shape=near_chi...]
    ppermute x1, starting transfers between devices: 3.38 us -> 1.91 us  [local(): relayed = lax.ppermute(back, 'cube', near)]
    ppermute x3, waiting for transfers between devices: 1.06 us -> 2.42 us  [local(): lax.ppermute(both, ('grp', 'cube'), relay_pairs((groups, members), step))]
    pallas_call x1, Pallas kernels: 4.02 us -> 3.21 us  [local(): pl.pallas_call(update_kernel, out_shape=(jax.ShapeDtypeStruct(rho.shape,...]
    ppermute x3, starting transfers between devices: 15.7 us -> 15.2 us  [local(): lax.ppermute(both, ('grp', 'cube'), relay_pairs((groups, members), step))]
    ppermute x1, waiting for transfers between devices: 0.01 us -> 0.44 us  [local(): shared = lax.ppermute(sent, 'cube', near)]
  transfers between devices with their start and end apart: 5 -> 5, of which waited for: 1 -> 2; matrix products, arithmetic and copies ran while one was open for 0% -> 0% of each run, Pallas kernels for 10% -> 7%
where the time goes in v2:
time: 40.3 us; the launch traced here: 40 us
  starting transfers between devices  23.3 us (58%)
  Pallas kernels  12.8 us (32%)
  waiting for transfers between devices  2.86 us (7%)
  between operations  0.8 us (2%)
    ppermute x3, starting transfers between devices, local(): lax.ppermute(both, ('grp', 'cube'), relay_pairs((groups, members), step))  15.2 us
    pallas_call x1, Pallas kernels, local(): pl.pallas_call(sums_kernel, out_shape=(near_chip((4, 64, 512)), near_chip...  6.88 us
    ppermute x1, starting transfers between devices, local(): shared = lax.ppermute(sent, 'cube', near)  6.14 us
    pallas_call x1, Pallas kernels, local(): pl.pallas_call(update_kernel, out_shape=(jax.ShapeDtypeStruct(rho.shape,...  3.21 us
    ppermute x3, waiting for transfers between devices, local(): lax.ppermute(both, ('grp', 'cube'), relay_pairs((groups, members), step))  2.42 us
    pallas_call x3, Pallas kernels, local(): pl.pallas_call(functools.partial(scatter_kernel, way), out_shape=near_chi...  2.31 us
    ppermute x1, starting transfers between devices, local(): relayed = lax.ppermute(back, 'cube', near)  1.91 us
  transfers between devices with their start and end apart: 5, of which 2 were waited for; matrix products, arithmetic and copies ran while one was open for 0% of the time, Pallas kernels for 7%

profile of v2, /device:TPU:1, one launch (start us, length us, event | category | flops | bytes accessed | tf_op | source)
XLA Modules:
  0.0 40.0 jit_solution(14081570847092290423)
XLA Ops:
  0.6 6.9 %sums_and_gather.1 = (f32[4,64,512]{2,1,0:T(8,128)S(1)}, bf16[528,512]{1,0:T(8,128)(2,1)S(1)}, f32[2,64,128]{2,1,0:T(8,128)S(1)}, f32[3,5,8,128]{3,2,1,0:T(8,128...) custom-call(f32[64,512]{1,0:T(8,128)} %bitcast.12, ...), custom_call_target="tpu_custom_call" | custom-call | tf_op jit(solution)/shard_map/sums_and_gather/pallas_call | solution.py:348
  7.5 6.1 %collective-permute-start = (f32[3,5,8,128]{3,2,1,0:T(8,128)S(1)}, f32[3,5,8,128]{3,2,1,0:T(8,128)S(1)}, u32[]{:S(2)}, u32[]{:S(2)}) collective-permute-start(f32[3,5,8,128]{3,2,1,0:T(8,128)S(1)} %get-tuple-element.15.mine.sent), channel_id=1, source_target_pairs={{0,1},{1,0},{2,3},{3,2},{4,5},{5,4},{6,7},{7,6},{8,9},{9,8},{10,11... | collective-permute-start | bytes 184328 | tf_op jit(solution)/shard_map/ppermute | solution.py:368
  13.7 0.2 shard_map.124.mine.own.near_own
  13.9 0.2 shard_map.122.far_own
  14.1 0.4 %collective-permute-done = f32[3,5,8,128]{3,2,1,0:T(8,128)S(1)} collective-permute-done((f32[3,5,8,128]{3,2,1,0:T(8,128)S(1)}, f32[3,5,8,128]{3,2,1,0:T(8,128)S(1)}, u32[]{:S(2)}, u32[]{:S(2)}) %collective-permute-start) | collective-permute-done | bytes 61472 | tf_op jit(solution)/shard_map/ppermute | solution.py:368
  14.6 8.1 %collective-permute-start.1 = (f32[2,5,8,128]{3,2,1,0:T(8,128)S(1)}, f32[2,5,8,128]{3,2,1,0:T(8,128)S(1)}, u32[]{:S(2)}, u32[]{:S(2)}) collective-permute-start(f32[2,5,8,128]{3,2,1,0:T(8,128)S(1)} %pad_maximum_fusion), channel_id=1, source_target_pairs={{0,32},{1,481},{2,34},{3,483},{4,36},{5,485},{6,38},{7,487},{8,40}... | collective-permute-start | bytes 122888 | tf_op jit(solution)/shard_map/ppermute | solution.py:385
  22.7 4.8 %collective-permute-start.2 = (f32[2,5,8,128]{3,2,1,0:T(8,128)S(1)}, f32[2,5,8,128]{3,2,1,0:T(8,128)S(1)}, u32[]{:S(2)}, u32[]{:S(2)}) collective-permute-start(f32[2,5,8,128]{3,2,1,0:T(8,128)S(1)} %pad_maximum_fusion.1), channel_id=1, source_target_pairs={{0,4},{1,17},{2,6},{3,19},{4,0},{5,21},{6,2},{7,23},{8,12},{9,25},... | collective-permute-start | bytes 122888 | tf_op jit(solution)/shard_map/ppermute | solution.py:385
  27.5 2.3 %collective-permute-start.3 = (f32[2,5,8,128]{3,2,1,0:T(8,128)S(1)}, f32[2,5,8,128]{3,2,1,0:T(8,128)S(1)}, u32[]{:S(2)}, u32[]{:S(2)}) collective-permute-start(f32[2,5,8,128]{3,2,1,0:T(8,128)S(1)} %pad_maximum_fusion.2), channel_id=1, source_target_pairs={{0,2},{1,9},{2,0},{3,11},{4,6},{5,13},{6,4},{7,15},{8,10},{9,1},{1... | collective-permute-start | bytes 122888 | tf_op jit(solution)/shard_map/ppermute | solution.py:385
  29.8 0.0 collective-permute-done.1.far.far_c
  29.9 0.0 collective-permute-done.2.far.far_a
  29.9 2.4 %collective-permute-done.3.far.far_b = f32[2,5,8,128]{3,2,1,0:T(8,128)S(1)} collective-permute-done((f32[2,5,8,128]{3,2,1,0:T(8,128)S(1)}, f32[2,5,8,128]{3,2,1,0:T(8,128)S(1)}, u32[]{:S(2)}, u32[]{:S(2)}) %collective-permute-start.3) | collective-permute-done | bytes 40992 | tf_op jit(solution)/shard_map/ppermute | solution.py:385
  32.3 1.9 %collective-permute-start.4 = (f32[4,5,8,128]{3,2,1,0:T(8,128)S(1)}, f32[4,5,8,128]{3,2,1,0:T(8,128)S(1)}, u32[]{:S(2)}, u32[]{:S(2)}) collective-permute-start(f32[4,5,8,128]{3,2,1,0:T(8,128)S(1)} %pack.1), channel_id=1, source_target_pairs={{0,1},{1,0},{2,3},{3,2},{4,5},{5,4},{6,7},{7,6},{8,9},{9,8},{10,11... | collective-permute-start | bytes 245768 | tf_op jit(solution)/shard_map/ppermute | solution.py:394
  34.2 0.8 %shard_map.123.steps = f32[4,64,512]{2,1,0:T(8,128)S(1)} custom-call(f32[4,64,512]{2,1,0:T(8,128)S(1)} %get-tuple-element.12.steps, s32[7,1,1024]{2,1,0:T(1,128)S(1)} %get-tuple-element.13.ids, s32[8,8,128]{2,1,0:T(8,128)S(1)} %get-tuple-element.14.counts, f32[3,5,8,128]{3,2,1,0:T(8,128)S(1)} %get-tuple-element.15.mine.sent, ...), custom_call_target="tpu_custom_call", output_to_operand_aliasing={{}: (0, {})} | custom-call | tf_op jit(solution)/shard_map/pallas_call | solution.py:397
  35.0 0.8 %shard_map.125.steps = f32[4,64,512]{2,1,0:T(8,128)S(1)} custom-call(f32[4,64,512]{2,1,0:T(8,128)S(1)} %shard_map.123.steps, s32[7,1,1024]{2,1,0:T(1,128)S(1)} %get-tuple-element.13.ids, s32[8,8,128]{2,1,0:T(8,128)S(1)} %get-tuple-element.14.counts, f32[3,5,8,128]{3,2,1,0:T(8,128)S(1)} %shard_map.124.mine.own.near_own, ...), custom_call_target="tpu_custom_call", output_to_operand_aliasing={{}: (0, {})} | custom-call | tf_op jit(solution)/shard_map/pallas_call | solution.py:397
  35.8 0.0 copy-start
  35.8 0.0 copy-start.1
  35.8 0.8 %shard_map.126.total = f32[4,64,512]{2,1,0:T(8,128)S(1)} custom-call(f32[4,64,512]{2,1,0:T(8,128)S(1)} %shard_map.125.steps, s32[7,1,1024]{2,1,0:T(1,128)S(1)} %get-tuple-element.13.ids, s32[8,8,128]{2,1,0:T(8,128)S(1)} %get-tuple-element.14.counts, f32[3,5,8,128]{3,2,1,0:T(8,128)S(1)} %shard_map.124.mine.own.near_own, ...), custom_call_target="tpu_custom_call", output_to_operand_aliasing={{}: (0, {})} | custom-call | tf_op jit(solution)/shard_map/pallas_call | solution.py:397
  36.6 0.0 collective-permute-done.4.relayed
  36.6 0.2 copy-done
  36.8 0.0 copy-done.1
  36.8 3.2 %scatter_and_update.1 = (f32[64,512]{1,0:T(8,128)}, f32[3,64,512]{2,1,0:T(8,128)}) custom-call(f32[64,512]{1,0:T(8,128)S(1)} %bitcast.13, f32[3,64,512]{2,1,0:T(8,128)S(1)} %bitcast.11, f32[4,64,512]{2,1,0:T(8,128)S(1)} %shard_map.126.total, s32[7,1,1024]{2,1,0:T(1,128)S(1)} %get-tuple-element.13.ids, s32[8,8,128]{2,1,0:T(8,128)S(1)} %get-tuple-element.14.counts, ...), custom_call_target="tpu_custom_call" | custom-call | tf_op jit(solution)/shard_map/scatter_and_update/pallas_call | solution.py:405
  (6 shorter events, 0.0 us)
Async XLA Ops:
  7.5 7.0 %collective-permute-start = (f32[3,5,8,128]{3,2,1,0:T(8,128)S(1)}, f32[3,5,8,128]{3,2,1,0:T(8,128)S(1)}, u32[]{:S(2)}, u32[]{:S(2)}) collective-permute-start(f32[3,5,8,128]{3,2,1,0:T(8,128)S(1)} %get-tuple-element.15.mine.sent), channel_id=1, source_target_pairs={{0,1},{1,0},{2,3},{3,2},{4,5},{5,4},{6,7},{7,6},{8,9},{9,8},{10,11... | collective-permute-start | bytes 184328 | tf_op jit(solution)/shard_map/ppermute | solution.py:368
  14.6 15.3 %collective-permute-start.1 = (f32[2,5,8,128]{3,2,1,0:T(8,128)S(1)}, f32[2,5,8,128]{3,2,1,0:T(8,128)S(1)}, u32[]{:S(2)}, u32[]{:S(2)}) collective-permute-start(f32[2,5,8,128]{3,2,1,0:T(8,128)S(1)} %pad_maximum_fusion), channel_id=1, source_target_pairs={{0,32},{1,481},{2,34},{3,483},{4,36},{5,485},{6,38},{7,487},{8,40}... | collective-permute-start | bytes 122888 | tf_op jit(solution)/shard_map/ppermute | solution.py:385
  22.7 7.2 %collective-permute-start.2 = (f32[2,5,8,128]{3,2,1,0:T(8,128)S(1)}, f32[2,5,8,128]{3,2,1,0:T(8,128)S(1)}, u32[]{:S(2)}, u32[]{:S(2)}) collective-permute-start(f32[2,5,8,128]{3,2,1,0:T(8,128)S(1)} %pad_maximum_fusion.1), channel_id=1, source_target_pairs={{0,4},{1,17},{2,6},{3,19},{4,0},{5,21},{6,2},{7,23},{8,12},{9,25},... | collective-permute-start | bytes 122888 | tf_op jit(solution)/shard_map/ppermute | solution.py:385
  27.5 4.7 %collective-permute-start.3 = (f32[2,5,8,128]{3,2,1,0:T(8,128)S(1)}, f32[2,5,8,128]{3,2,1,0:T(8,128)S(1)}, u32[]{:S(2)}, u32[]{:S(2)}) collective-permute-start(f32[2,5,8,128]{3,2,1,0:T(8,128)S(1)} %pad_maximum_fusion.2), channel_id=1, source_target_pairs={{0,2},{1,9},{2,0},{3,11},{4,6},{5,13},{6,4},{7,15},{8,10},{9,1},{1... | collective-permute-start | bytes 122888 | tf_op jit(solution)/shard_map/ppermute | solution.py:385
  32.3 4.3 %collective-permute-start.4 = (f32[4,5,8,128]{3,2,1,0:T(8,128)S(1)}, f32[4,5,8,128]{3,2,1,0:T(8,128)S(1)}, u32[]{:S(2)}, u32[]{:S(2)}) collective-permute-start(f32[4,5,8,128]{3,2,1,0:T(8,128)S(1)} %pack.1), channel_id=1, source_target_pairs={{0,1},{1,0},{2,3},{3,2},{4,5},{5,4},{6,7},{7,6},{8,9},{9,8},{10,11... | collective-permute-start | bytes 245768 | tf_op jit(solution)/shard_map/ppermute | solution.py:394
  35.8 1.0 %copy-start = (f32[1,1,3,64,512]{4,3,2,1,0:T(8,128)S(1)}, f32[1,1,3,64,512]{4,3,2,1,0:T(8,128)}, u32[]{:S(2)}) copy-start(f32[1,1,3,64,512]{4,3,2,1,0:T(8,128)} %param.12) | copy-start | bytes 1179652
  35.8 1.0 %copy-start.1 = (f32[1,1,64,512]{3,2,1,0:T(8,128)S(1)}, f32[1,1,64,512]{3,2,1,0:T(8,128)}, u32[]{:S(2)}) copy-start(f32[1,1,64,512]{3,2,1,0:T(8,128)} %param.11) | copy-start | bytes 393220

commit v3 on v2

--- a/solution.py
+++ b/solution.py
@@ -73,14 +73,21 @@
     _, weights, derivative = gll_tables()
     along_second = np.kron(np.eye(4), np.kron(derivative, np.eye(8))).T
     along_third = np.kron(np.eye(32), derivative).T
-    first = np.zeros((32, 128), np.float32)
-    for t in range(4):
-        for s in range(4):
-            for r in range(2):
-                for half in range(2):
-                    factor = derivative[2 * t + half, 2 * s + (half ^ r)]
-                    first[8 * t + 2 * s + r, 64 * half : 64 * half + 64] = factor
-    inner = np.stack(bf16_parts(along_second, 2) + bf16_parts(along_third, 2))
+    first = np.zeros((16, 128), np.float32)
+    for p in range(2):
+        for t in range(2):
+            for s in range(2):
+                for r in range(2):
+                    for half in range(2):
+                        a, c = 2 * t + half, 2 * s + (half ^ r)
+                        factor = derivative[a, c] + (-1) ** p * derivative[a, 7 - c]
+                        row = 8 * p + 4 * t + 2 * s + r
+                        first[row, 64 * half : 64 * half + 64] = factor / 2
+    inner = []
+    for table in (along_second, along_third):
+        big, small = bf16_parts(table, 2)
+        inner += [big, big, small]
+    inner = np.concatenate(inner, axis=0)
     node = np.kron(weights, np.kron(weights, weights)).astype(np.float32)[None]
     node_parts = np.concatenate(
         bf16_parts(node, 3) + [np.zeros((13, 512), np.float32).astype(BF16)], axis=0
@@ -212,26 +219,30 @@
 
     def along_first(part):
         tiles = [part[:, 128 * t : 128 * t + 128] for t in range(4)]
-        swapped = [pltpu.roll(tile, 64, 1) for tile in tiles]
+        mirror = [pltpu.roll(tiles[3 - t], 64, 1) for t in range(2)]
         outs = []
-        for t in range(4):
-            out = None
-            for s in range(4):
-                for r, tile in enumerate((tiles[s], swapped[s])):
-                    at = 8 * t + 2 * s + r
-                    term = tile * first[at : at + 1, :]
-                    out = term if out is None else out + term
-            outs.append(out)
-        return jnp.concatenate(outs, axis=1)
-
-    halves = [None, None]
-    for d in (1, 2):
-        high, low = split(jnp.concatenate(flux(d), axis=0))
-        big, small = inner[2 * d - 2], inner[2 * d - 1]
-        for k in range(2):
-            lanes = slice(256 * k, 256 * k + 256)
-            half = dot(high[:, lanes], big) + dot(low[:, lanes], big) + dot(high[:, lanes], small)
-            halves[k] = half if halves[k] is None else halves[k] + half
+        for p in range(2):
+            halves = [tiles[t] - mirror[t] if p else tiles[t] + mirror[t] for t in range(2)]
+            swapped = [pltpu.roll(half, 64, 1) for half in halves]
+            outs.append([])
+            for t in range(2):
+                out = None
+                for s in range(2):
+                    for r, tile in enumerate((halves[s], swapped[s])):
+                        at = 8 * p + 4 * t + 2 * s + r
+                        term = tile * first[at : at + 1, :]
+                        out = term if out is None else out + term
+                outs[p].append(out)
+        head = [outs[0][t] + outs[1][t] for t in range(2)]
+        tail = [pltpu.roll(outs[1][t] - outs[0][t], 64, 1) for t in range(2)]
+        return jnp.concatenate(head + tail[::-1], axis=1)
+
+    parts = [split(jnp.concatenate(flux(d), axis=0)) for d in (1, 2)]
+    halves = []
+    for k in range(2):
+        lanes = slice(256 * k, 256 * k + 256)
+        deep = [part[:, lanes] for high, low in parts for part in (high, low, high)]
+        halves.append(dot(jnp.concatenate(deep, axis=1), inner[...]))
     fluxes = flux(0)
     change = jnp.concatenate(halves, axis=1)
     node_w = node[...]
@@ -276,9 +287,14 @@
     back[3] = own[2]
 
 
-def scatter_kernel(way, steps, ids, counts, mine, far, total):
-    row = ARRIVING[way]
-    added = spread(ids[row], counts[row], mine[way], far[0])
+def scatter_kernel(ways, steps, ids, counts, sent, near_own, *fars_and_total):
+    fars, total = fars_and_total[:-1], fars_and_total[-1]
+    added = None
+    for way, far in zip(ways, fars):
+        row = ARRIVING[way]
+        mine = sent[2] if way == 2 else near_own[way]
+        more = spread(ids[row], counts[row], mine, far[0])
+        added = more if added is None else added + more
     for f in range(4):
         total[f] = steps[f] + added[64 * f : 64 * f + 64]
 
@@ -393,14 +409,17 @@
     )(*far, on_chip(near_own))
     relayed = lax.ppermute(back, "cube", near)
     total = steps
-    for way in (2, 0, 1):
+    for ways in ((2, 0), (1,)):
         total = pl.pallas_call(
-            functools.partial(scatter_kernel, way),
+            functools.partial(scatter_kernel, ways),
             out_shape=near_chip((4, 64, 512)),
-            in_specs=[whole] * 5,
+            in_specs=[whole] * (5 + len(ways)),
             out_specs=whole,
             input_output_aliases={0: 0},
-        )(on_chip(total), *plan, on_chip(sent if way == 2 else near_own), far[way])
+        )(
+            on_chip(total), *plan, on_chip(sent), on_chip(near_own),
+            *[far[way] for way in ways],
+        )
     hbm = pl.BlockSpec(memory_space=pl.ANY)
     new_density, new_momentum = pl.pallas_call(
         update_kernel,

time: 40.3 us -> 39.9 us (0.990)
    pallas_call x3 -> x2, Pallas kernels: 2.31 us -> 2.08 us  [local(): pl.pallas_call(functools.partial(scatter_kernel, ways), out_shape=near_ch...]
  transfers between devices with their start and end apart: 5 -> 5, of which waited for: 2 -> 2; matrix products, arithmetic and copies ran while one was open for 0% -> 0% of each run, Pallas kernels for 7% -> 6%
where the time goes in v3:
time: 39.9 us; the launch traced here: 39.6 us
  starting transfers between devices  23.3 us (58%)
  Pallas kernels  12.5 us (31%)
  waiting for transfers between devices  2.86 us (7%)
  between operations  0.79 us (2%)
    ppermute x3, starting transfers between devices, local(): lax.ppermute(both, ('grp', 'cube'), relay_pairs((groups, members), step))  15.2 us
    pallas_call x1, Pallas kernels, local(): pl.pallas_call(sums_kernel, out_shape=(near_chip((4, 64, 512)), near_chip...  6.75 us
    ppermute x1, starting transfers between devices, local(): shared = lax.ppermute(sent, 'cube', near)  6.13 us
    pallas_call x1, Pallas kernels, local(): pl.pallas_call(update_kernel, out_shape=(jax.ShapeDtypeStruct(rho.shape,...  3.22 us
    ppermute x3, waiting for transfers between devices, local(): lax.ppermute(both, ('grp', 'cube'), relay_pairs((groups, members), step))  2.42 us
    pallas_call x2, Pallas kernels, local(): pl.pallas_call(functools.partial(scatter_kernel, ways), out_shape=near_ch...  2.08 us
    ppermute x1, starting transfers between devices, local(): relayed = lax.ppermute(back, 'cube', near)  1.91 us
  transfers between devices with their start and end apart: 5, of which 2 were waited for; matrix products, arithmetic and copies ran while one was open for 0% of the time, Pallas kernels for 6%

profile of v3, /device:TPU:1, one launch (start us, length us, event | category | flops | bytes accessed | tf_op | source)
XLA Modules:
  0.0 39.6 jit_solution(1676724402213012785)
XLA Ops:
  0.6 6.8 %sums_and_gather.1 = (f32[4,64,512]{2,1,0:T(8,128)S(1)}, bf16[528,512]{1,0:T(8,128)(2,1)S(1)}, f32[2,64,128]{2,1,0:T(8,128)S(1)}, f32[3,5,8,128]{3,2,1,0:T(8,128...) custom-call(f32[64,512]{1,0:T(8,128)} %bitcast.12, ...), custom_call_target="tpu_custom_call" | custom-call | tf_op jit(solution)/shard_map/sums_and_gather/pallas_call | solution.py:364
  7.4 6.1 %collective-permute-start = (f32[3,5,8,128]{3,2,1,0:T(8,128)S(1)}, f32[3,5,8,128]{3,2,1,0:T(8,128)S(1)}, u32[]{:S(2)}, u32[]{:S(2)}) collective-permute-start(f32[3,5,8,128]{3,2,1,0:T(8,128)S(1)} %get-tuple-element.15.sent), channel_id=1, source_target_pairs={{0,1},{1,0},{2,3},{3,2},{4,5},{5,4},{6,7},{7,6},{8,9},{9,8},{10,11... | collective-permute-start | bytes 184328 | tf_op jit(solution)/shard_map/ppermute | solution.py:384
  13.5 0.2 shard_map.122.near_own.own
  13.8 0.2 shard_map.123.far_own
  14.0 0.4 %collective-permute-done = f32[3,5,8,128]{3,2,1,0:T(8,128)S(1)} collective-permute-done((f32[3,5,8,128]{3,2,1,0:T(8,128)S(1)}, f32[3,5,8,128]{3,2,1,0:T(8,128)S(1)}, u32[]{:S(2)}, u32[]{:S(2)}) %collective-permute-start) | collective-permute-done | bytes 61472 | tf_op jit(solution)/shard_map/ppermute | solution.py:384
  14.4 8.1 %collective-permute-start.1 = (f32[2,5,8,128]{3,2,1,0:T(8,128)S(1)}, f32[2,5,8,128]{3,2,1,0:T(8,128)S(1)}, u32[]{:S(2)}, u32[]{:S(2)}) collective-permute-start(f32[2,5,8,128]{3,2,1,0:T(8,128)S(1)} %pad_maximum_fusion), channel_id=1, source_target_pairs={{0,32},{1,481},{2,34},{3,483},{4,36},{5,485},{6,38},{7,487},{8,40}... | collective-permute-start | bytes 122888 | tf_op jit(solution)/shard_map/ppermute | solution.py:401
  22.6 4.8 %collective-permute-start.2 = (f32[2,5,8,128]{3,2,1,0:T(8,128)S(1)}, f32[2,5,8,128]{3,2,1,0:T(8,128)S(1)}, u32[]{:S(2)}, u32[]{:S(2)}) collective-permute-start(f32[2,5,8,128]{3,2,1,0:T(8,128)S(1)} %pad_maximum_fusion.1), channel_id=1, source_target_pairs={{0,4},{1,17},{2,6},{3,19},{4,0},{5,21},{6,2},{7,23},{8,12},{9,25},... | collective-permute-start | bytes 122888 | tf_op jit(solution)/shard_map/ppermute | solution.py:401
  27.4 2.3 %collective-permute-start.3 = (f32[2,5,8,128]{3,2,1,0:T(8,128)S(1)}, f32[2,5,8,128]{3,2,1,0:T(8,128)S(1)}, u32[]{:S(2)}, u32[]{:S(2)}) collective-permute-start(f32[2,5,8,128]{3,2,1,0:T(8,128)S(1)} %pad_maximum_fusion.2), channel_id=1, source_target_pairs={{0,2},{1,9},{2,0},{3,11},{4,6},{5,13},{6,4},{7,15},{8,10},{9,1},{1... | collective-permute-start | bytes 122888 | tf_op jit(solution)/shard_map/ppermute | solution.py:401
  29.7 0.0 collective-permute-done.1.fars_and_total_0_.far_c
  29.7 0.0 collective-permute-done.2.fars_and_total_1_.far_a
  29.7 2.4 %collective-permute-done.3.fars_and_total_0_.far_b = f32[2,5,8,128]{3,2,1,0:T(8,128)S(1)} collective-permute-done((f32[2,5,8,128]{3,2,1,0:T(8,128)S(1)}, f32[2,5,8,128]{3,2,1,0:T(8,128)S(1)}, u32[]{:S(2)}, u32[]{:S(2)}) %collective-permute-start.3) | collective-permute-done | bytes 40992 | tf_op jit(solution)/shard_map/ppermute | solution.py:401
  32.1 1.9 %collective-permute-start.4 = (f32[4,5,8,128]{3,2,1,0:T(8,128)S(1)}, f32[4,5,8,128]{3,2,1,0:T(8,128)S(1)}, u32[]{:S(2)}, u32[]{:S(2)}) collective-permute-start(f32[4,5,8,128]{3,2,1,0:T(8,128)S(1)} %pack.1), channel_id=1, source_target_pairs={{0,1},{1,0},{2,3},{3,2},{4,5},{5,4},{6,7},{7,6},{8,9},{9,8},{10,11... | collective-permute-start | bytes 245768 | tf_op jit(solution)/shard_map/ppermute | solution.py:410
  34.1 1.3 %shard_map.124.steps = f32[4,64,512]{2,1,0:T(8,128)S(1)} custom-call(f32[4,64,512]{2,1,0:T(8,128)S(1)} %get-tuple-element.12.steps, s32[7,1,1024]{2,1,0:T(1,128)S(1)} %get-tuple-element.13.ids, s32[8,8,128]{2,1,0:T(8,128)S(1)} %get-tuple-element.14.counts, f32[3,5,8,128]{3,2,1,0:T(8,128)S(1)} %get-tuple-element.15.sent, ...), custom_call_target="tpu_custom_call", output_to_operand_aliasing={{}: (0, {})} | custom-call | tf_op jit(solution)/shard_map/pallas_call | solution.py:413
  35.4 0.0 copy-start
  35.4 0.0 copy-start.1
  35.4 0.8 %shard_map.125.total = f32[4,64,512]{2,1,0:T(8,128)S(1)} custom-call(f32[4,64,512]{2,1,0:T(8,128)S(1)} %shard_map.124.steps, s32[7,1,1024]{2,1,0:T(1,128)S(1)} %get-tuple-element.13.ids, s32[8,8,128]{2,1,0:T(8,128)S(1)} %get-tuple-element.14.counts, f32[3,5,8,128]{3,2,1,0:T(8,128)S(1)} %get-tuple-element.15.sent, ...), custom_call_target="tpu_custom_call", output_to_operand_aliasing={{}: (0, {})} | custom-call | tf_op jit(solution)/shard_map/pallas_call | solution.py:413
  36.2 0.0 collective-permute-done.4.relayed
  36.2 0.2 copy-done
  36.4 0.0 copy-done.1
  36.4 3.2 %scatter_and_update.1 = (f32[64,512]{1,0:T(8,128)}, f32[3,64,512]{2,1,0:T(8,128)}) custom-call(f32[64,512]{1,0:T(8,128)S(1)} %bitcast.13, f32[3,64,512]{2,1,0:T(8,128)S(1)} %bitcast.11, f32[4,64,512]{2,1,0:T(8,128)S(1)} %shard_map.125.total, s32[7,1,1024]{2,1,0:T(1,128)S(1)} %get-tuple-element.13.ids, s32[8,8,128]{2,1,0:T(8,128)S(1)} %get-tuple-element.14.counts, ...), custom_call_target="tpu_custom_call" | custom-call | tf_op jit(solution)/shard_map/scatter_and_update/pallas_call | solution.py:424
  (6 shorter events, 0.0 us)
Async XLA Ops:
  7.4 7.0 %collective-permute-start = (f32[3,5,8,128]{3,2,1,0:T(8,128)S(1)}, f32[3,5,8,128]{3,2,1,0:T(8,128)S(1)}, u32[]{:S(2)}, u32[]{:S(2)}) collective-permute-start(f32[3,5,8,128]{3,2,1,0:T(8,128)S(1)} %get-tuple-element.15.sent), channel_id=1, source_target_pairs={{0,1},{1,0},{2,3},{3,2},{4,5},{5,4},{6,7},{7,6},{8,9},{9,8},{10,11... | collective-permute-start | bytes 184328 | tf_op jit(solution)/shard_map/ppermute | solution.py:384
  14.4 15.3 %collective-permute-start.1 = (f32[2,5,8,128]{3,2,1,0:T(8,128)S(1)}, f32[2,5,8,128]{3,2,1,0:T(8,128)S(1)}, u32[]{:S(2)}, u32[]{:S(2)}) collective-permute-start(f32[2,5,8,128]{3,2,1,0:T(8,128)S(1)} %pad_maximum_fusion), channel_id=1, source_target_pairs={{0,32},{1,481},{2,34},{3,483},{4,36},{5,485},{6,38},{7,487},{8,40}... | collective-permute-start | bytes 122888 | tf_op jit(solution)/shard_map/ppermute | solution.py:401
  22.6 7.2 %collective-permute-start.2 = (f32[2,5,8,128]{3,2,1,0:T(8,128)S(1)}, f32[2,5,8,128]{3,2,1,0:T(8,128)S(1)}, u32[]{:S(2)}, u32[]{:S(2)}) collective-permute-start(f32[2,5,8,128]{3,2,1,0:T(8,128)S(1)} %pad_maximum_fusion.1), channel_id=1, source_target_pairs={{0,4},{1,17},{2,6},{3,19},{4,0},{5,21},{6,2},{7,23},{8,12},{9,25},... | collective-permute-start | bytes 122888 | tf_op jit(solution)/shard_map/ppermute | solution.py:401
  27.4 4.7 %collective-permute-start.3 = (f32[2,5,8,128]{3,2,1,0:T(8,128)S(1)}, f32[2,5,8,128]{3,2,1,0:T(8,128)S(1)}, u32[]{:S(2)}, u32[]{:S(2)}) collective-permute-start(f32[2,5,8,128]{3,2,1,0:T(8,128)S(1)} %pad_maximum_fusion.2), channel_id=1, source_target_pairs={{0,2},{1,9},{2,0},{3,11},{4,6},{5,13},{6,4},{7,15},{8,10},{9,1},{1... | collective-permute-start | bytes 122888 | tf_op jit(solution)/shard_map/ppermute | solution.py:401
  32.1 4.0 %collective-permute-start.4 = (f32[4,5,8,128]{3,2,1,0:T(8,128)S(1)}, f32[4,5,8,128]{3,2,1,0:T(8,128)S(1)}, u32[]{:S(2)}, u32[]{:S(2)}) collective-permute-start(f32[4,5,8,128]{3,2,1,0:T(8,128)S(1)} %pack.1), channel_id=1, source_target_pairs={{0,1},{1,0},{2,3},{3,2},{4,5},{5,4},{6,7},{7,6},{8,9},{9,8},{10,11... | collective-permute-start | bytes 245768 | tf_op jit(solution)/shard_map/ppermute | solution.py:410
  35.4 1.0 %copy-start = (f32[1,1,3,64,512]{4,3,2,1,0:T(8,128)S(1)}, f32[1,1,3,64,512]{4,3,2,1,0:T(8,128)}, u32[]{:S(2)}) copy-start(f32[1,1,3,64,512]{4,3,2,1,0:T(8,128)} %param.12) | copy-start | bytes 1179652
  35.4 1.0 %copy-start.1 = (f32[1,1,64,512]{3,2,1,0:T(8,128)S(1)}, f32[1,1,64,512]{3,2,1,0:T(8,128)}, u32[]{:S(2)}) copy-start(f32[1,1,64,512]{3,2,1,0:T(8,128)} %param.11) | copy-start | bytes 393220

commit v4 on v3

--- a/solution.py
+++ b/solution.py
@@ -264,21 +264,59 @@
     volumes[1] = pltpu.roll(volumes[0], 1, 0)
 
     make_plan(section, cross, section_n, cross_n, code, ids, counts)
-    for j, row in enumerate(OTHERS):
-        pick(table, volumes, ids[row], counts[row], send, j)
-
-    @pl.when(code[0] >= 2)
+    pick(table, volumes, ids[OTHERS[2]], counts[OTHERS[2]], send, 2)
+
+    @pl.when(code[0] < 4)
+    def _():
+        for j in range(2):
+            pick(table, volumes, ids[OTHERS[j]], counts[OTHERS[j]], send, j)
+
+    @pl.when(code[0] >= 4)
+    def _():
+        for j in range(2):
+            send[j] = jnp.zeros((5, 8, 128), F32)
+
+    @pl.when(code[0] & 2 == 2)
     def _():
         pick(table, volumes, ids[FAR], counts[FAR], far_own, 0)
         for j, row in enumerate(NEAR):
             pick(table, volumes, ids[row], counts[row], near_own, j)
 
 
-def late_kernel(rows, table, volumes, ids, counts, before, own):
-    @pl.when(jnp.max(counts[7]) < 2)
-    def _():
-        for j, row in enumerate(rows):
+def far_kernel(table, volumes, ids, counts, before, own):
+    @pl.when(jnp.max(counts[7]) & 2 == 0)
+    def _():
+        pick(table, volumes, ids[FAR], counts[FAR], own, 0)
+
+
+def near_kernel(table, volumes, ids, counts, before, own, rest):
+    code = jnp.max(counts[7])
+
+    @pl.when(code & 2 == 0)
+    def _():
+        for j, row in enumerate(NEAR):
             pick(table, volumes, ids[row], counts[row], own, j)
+
+    @pl.when(code >= 4)
+    def _():
+        for j in range(2):
+            pick(table, volumes, ids[OTHERS[j]], counts[OTHERS[j]], rest, j)
+
+    @pl.when(code < 4)
+    def _():
+        for j in range(2):
+            rest[j] = jnp.zeros((5, 8, 128), F32)
+
+
+def pack_far_kernel(own, shared, both):
+    both[0] = own[0]
+    both[1] = shared[2]
+
+
+def pack_near_kernel(own, shared, late_shared, *both):
+    for j in range(2):
+        both[j][0] = own[j]
+        both[j][1] = shared[j] + late_shared[j]
 
 
 def pack_kernel(far_a, far_b, far_c, own, back):
@@ -300,10 +338,10 @@
 
 
 def update_kernel(
-    density, momentum, total, ids, counts, sent, near_own, far_own, relayed, new_density,
+    density, momentum, total, ids, counts, sent, rest, near_own, far_own, relayed, new_density,
     new_momentum, ready, arrived,
 ):
-    mine = (sent[0], sent[1], far_own[0], near_own[2])
+    mine = (sent[0] + rest[0], sent[1] + rest[1], far_own[0], near_own[2])
     added = None
     for j, row in enumerate(RELAYED):
         more = spread(ids[row], counts[row], mine[j], relayed[j])
@@ -349,7 +387,8 @@
     groups = lax.axis_size("grp")
     device = lax.axis_index("grp") * members + lax.axis_index("cube")
     early = jnp.logical_and(device > 0, device < members)
-    code = ((device & 1) + 2 * early.astype(jnp.int32)).reshape(1)
+    late = device >= (groups - 1) * members
+    code = ((device & 1) + jnp.where(early, 2, jnp.where(late, 4, 0))).reshape(1)
     whole = pl.BlockSpec(memory_space=pltpu.VMEM)
     scalars = pl.BlockSpec(memory_space=pltpu.SMEM)
     near = [(i, i ^ 1) for i in range(members)]
@@ -383,23 +422,40 @@
     plan = (on_chip(ids), on_chip(counts))
     shared = lax.ppermute(sent, "cube", near)
 
-    def gather(rows, own):
+    def gather(kernel, own, *more):
         return pl.pallas_call(
-            functools.partial(late_kernel, rows),
-            out_shape=near_chip(own.shape),
+            kernel,
+            out_shape=(near_chip(own.shape),) + more,
             in_specs=[whole] * 5,
-            out_specs=whole,
+            out_specs=(whole,) * (1 + len(more)),
             input_output_aliases={4: 0},
         )(on_chip(table), on_chip(volumes), *plan, on_chip(own))
 
-    far_own = gather((FAR,), far_own)
-    near_own = gather(NEAR, near_own)
-    far = [None] * 3
-    for step in range(3):
-        own = far_own[0] if step == 2 else near_own[step]
-        both = jnp.stack([own, shared[step]])
+    (far_own,) = gather(far_kernel, far_own)
+    near_own, rest = gather(near_kernel, near_own, near_chip((2,) + section_sums))
+    last = (groups - 1) * members
+    late_shared = lax.ppermute(
+        rest, ("grp", "cube"), [(last + m, last + (m ^ 1)) for m in range(members)]
+    )
+    pair = near_chip((2,) + section_sums)
+    far_both = pl.pallas_call(
+        pack_far_kernel,
+        out_shape=pair,
+        in_specs=[whole] * 2,
+        out_specs=whole,
+        name="pack_far",
+    )(on_chip(far_own), on_chip(shared))
+    near_both = pl.pallas_call(
+        pack_near_kernel,
+        out_shape=(pair, pair),
+        in_specs=[whole] * 3,
+        out_specs=(whole, whole),
+        name="pack_near",
+    )(on_chip(near_own), on_chip(shared), on_chip(late_shared))
+    far = []
+    for step, both in enumerate((*near_both, far_both)):
         part = lax.ppermute(both, ("grp", "cube"), relay_pairs((groups, members), step))
-        far[step] = on_chip(part)
+        far.append(on_chip(part))
     back = pl.pallas_call(
         pack_kernel,
         out_shape=near_chip((4,) + section_sums),
@@ -427,13 +483,13 @@
             jax.ShapeDtypeStruct(rho.shape, F32),
             jax.ShapeDtypeStruct(mom.shape, F32),
         ),
-        in_specs=[whole] * 9,
+        in_specs=[whole] * 10,
         out_specs=(hbm, hbm),
         scratch_shapes=[pltpu.VMEM((4, 64, 512), F32), pltpu.SemaphoreType.DMA((4,))],
         name="scatter_and_update",
     )(
-        on_chip(rho), on_chip(mom), on_chip(total), *plan, on_chip(sent), on_chip(near_own),
-        on_chip(far_own), on_chip(relayed),
+        on_chip(rho), on_chip(mom), on_chip(total), *plan, on_chip(sent), on_chip(rest),
+        on_chip(near_own), on_chip(far_own), on_chip(relayed),
     )
     return (new_density[None, None], new_momentum[None, None])
 

time: 39.9 us -> 42.7 us (1.070)
  starting transfers between devices: 23.3 us -> 27.6 us
  waiting for transfers between devices: 2.86 us -> 1.07 us
    ppermute x3, starting transfers between devices: 15.2 us -> 17.1 us  [local(): lax.ppermute(both, ('grp', 'cube'), relay_pairs((groups, members), step))]
    ppermute x1, starting transfers between devices: 1.91 us -> 3.68 us  [local(): relayed = lax.ppermute(back, 'cube', near)]
    ppermute x3, waiting for transfers between devices: 2.42 us -> 1.06 us  [local(): lax.ppermute(both, ('grp', 'cube'), relay_pairs((groups, members), step))]
    ppermute x0 -> x1, starting transfers between devices: none -> 0.66 us  [local(): lax.ppermute(rest, ('grp', 'cube'), [(last + m, last + (m ^ 1)) for m in...]
    ppermute x1, waiting for transfers between devices: 0.44 us -> 0.01 us  [local(): shared = lax.ppermute(sent, 'cube', near)]
  transfers between devices with their start and end apart: 5 -> 6, of which waited for: 2 -> 1; matrix products, arithmetic and copies ran while one was open for 0% -> 0% of each run, Pallas kernels for 6% -> 6%
where the time goes in v4:
time: 42.7 us; the launch traced here: 42.4 us
  starting transfers between devices  27.6 us (65%)
  Pallas kernels  12.7 us (30%)
  waiting for transfers between devices  1.07 us (3%)
  between operations  0.81 us (2%)
    ppermute x3, starting transfers between devices, local(): lax.ppermute(both, ('grp', 'cube'), relay_pairs((groups, members), step))  17.1 us
    pallas_call x1, Pallas kernels, local(): pl.pallas_call(sums_kernel, out_shape=(near_chip((4, 64, 512)), near_chip...  7 us
    ppermute x1, starting transfers between devices, local(): shared = lax.ppermute(sent, 'cube', near)  6.1 us
    ppermute x1, starting transfers between devices, local(): relayed = lax.ppermute(back, 'cube', near)  3.68 us
    pallas_call x1, Pallas kernels, local(): pl.pallas_call(update_kernel, out_shape=(jax.ShapeDtypeStruct(rho.shape,...  3.21 us
    pallas_call x2, Pallas kernels, local(): pl.pallas_call(functools.partial(scatter_kernel, ways), out_shape=near_ch...  2.08 us
    ppermute x3, waiting for transfers between devices, local(): lax.ppermute(both, ('grp', 'cube'), relay_pairs((groups, members), step))  1.06 us
  transfers between devices with their start and end apart: 6, of which 1 were waited for; matrix products, arithmetic and copies ran while one was open for 0% of the time, Pallas kernels for 6%

profile of v4, /device:TPU:1, one launch (start us, length us, event | category | flops | bytes accessed | tf_op | source)
XLA Modules:
  0.0 42.4 jit_solution(3653811362440128304)
XLA Ops:
  0.6 7.0 %sums_and_gather.1 = (f32[4,64,512]{2,1,0:T(8,128)S(1)}, bf16[528,512]{1,0:T(8,128)(2,1)S(1)}, f32[2,64,128]{2,1,0:T(8,128)S(1)}, f32[3,5,8,128]{3,2,1,0:T(8,128...) custom-call(f32[64,512]{1,0:T(8,128)} %bitcast.12, ...), custom_call_target="tpu_custom_call" | custom-call | tf_op jit(solution)/shard_map/sums_and_gather/pallas_call | solution.py:403
  7.7 6.1 %collective-permute-start = (f32[3,5,8,128]{3,2,1,0:T(8,128)S(1)}, f32[3,5,8,128]{3,2,1,0:T(8,128)S(1)}, u32[]{:S(2)}, u32[]{:S(2)}) collective-permute-start(f32[3,5,8,128]{3,2,1,0:T(8,128)S(1)} %get-tuple-element.19.sent), channel_id=1, source_target_pairs={{0,1},{1,0},{2,3},{3,2},{4,5},{5,4},{6,7},{7,6},{8,9},{9,8},{10,11... | collective-permute-start | bytes 184328 | tf_op jit(solution)/shard_map/ppermute | solution.py:423
  13.8 0.2 shard_map.122
  14.0 0.7 %collective-permute-start.2 = (f32[2,5,8,128]{3,2,1,0:T(8,128)S(1)}, f32[2,5,8,128]{3,2,1,0:T(8,128)S(1)}, u32[]{:S(2)}, u32[]{:S(2)}) collective-permute-start(f32[2,5,8,128]{3,2,1,0:T(8,128)S(1)} %get-tuple-element.25.rest), channel_id=1, source_target_pairs={{480,481},{481,480},{482,483},{483,482},{484,485},{485,484},{486,4... | collective-permute-start | bytes 122888 | tf_op jit(solution)/shard_map/ppermute | solution.py:437
  14.7 0.2 shard_map.123.own.far_own
  14.9 0.0 collective-permute-done.2.late_shared
  14.9 0.0 collective-permute-done.shared
  14.9 2.1 %collective-permute-start.3 = (f32[2,5,8,128]{3,2,1,0:T(8,128)S(1)}, f32[2,5,8,128]{3,2,1,0:T(8,128)S(1)}, u32[]{:S(2)}, u32[]{:S(2)}) collective-permute-start(f32[2,5,8,128]{3,2,1,0:T(8,128)S(1)} %get-tuple-element.26), channel_id=1, source_target_pairs={{0,4},{1,17},{2,6},{3,19},{4,0},{5,21},{6,2},{7,23},{8,12},{9,25},... | collective-permute-start | bytes 122888 | tf_op jit(solution)/shard_map/ppermute | solution.py:457
  17.0 2.3 %collective-permute-start.4 = (f32[2,5,8,128]{3,2,1,0:T(8,128)S(1)}, f32[2,5,8,128]{3,2,1,0:T(8,128)S(1)}, u32[]{:S(2)}, u32[]{:S(2)}) collective-permute-start(f32[2,5,8,128]{3,2,1,0:T(8,128)S(1)} %get-tuple-element.27), channel_id=1, source_target_pairs={{0,2},{1,9},{2,0},{3,11},{4,6},{5,13},{6,4},{7,15},{8,10},{9,1},{1... | collective-permute-start | bytes 122888 | tf_op jit(solution)/shard_map/ppermute | solution.py:457
  19.4 12.7 %collective-permute-start.1 = (f32[2,5,8,128]{3,2,1,0:T(8,128)S(1)}, f32[2,5,8,128]{3,2,1,0:T(8,128)S(1)}, u32[]{:S(2)}, u32[]{:S(2)}) collective-permute-start(f32[2,5,8,128]{3,2,1,0:T(8,128)S(1)} %pack_far.1), channel_id=1, source_target_pairs={{0,32},{1,481},{2,34},{3,483},{4,36},{5,485},{6,38},{7,487},{8,40}... | collective-permute-start | bytes 122888 | tf_op jit(solution)/shard_map/ppermute | solution.py:457
  32.0 0.0 collective-permute-done.3.fars_and_total_1_.far_a
  32.1 0.0 collective-permute-done.4.fars_and_total_0_.far_b
  32.1 1.1 %collective-permute-done.1.fars_and_total_0_.far_c = f32[2,5,8,128]{3,2,1,0:T(8,128)S(1)} collective-permute-done((f32[2,5,8,128]{3,2,1,0:T(8,128)S(1)}, f32[2,5,8,128]{3,2,1,0:T(8,128)S(1)}, u32[]{:S(2)}, u32[]{:S(2)}) %collective-permute-start.1) | collective-permute-done | bytes 40992 | tf_op jit(solution)/shard_map/ppermute | solution.py:457
  33.1 3.7 %collective-permute-start.5 = (f32[4,5,8,128]{3,2,1,0:T(8,128)S(1)}, f32[4,5,8,128]{3,2,1,0:T(8,128)S(1)}, u32[]{:S(2)}, u32[]{:S(2)}) collective-permute-start(f32[4,5,8,128]{3,2,1,0:T(8,128)S(1)} %pack.1), channel_id=1, source_target_pairs={{0,1},{1,0},{2,3},{3,2},{4,5},{5,4},{6,7},{7,6},{8,9},{9,8},{10,11... | collective-permute-start | bytes 245768 | tf_op jit(solution)/shard_map/ppermute | solution.py:466
  36.8 1.3 %shard_map.124.steps = f32[4,64,512]{2,1,0:T(8,128)S(1)} custom-call(f32[4,64,512]{2,1,0:T(8,128)S(1)} %get-tuple-element.16.steps, s32[7,1,1024]{2,1,0:T(1,128)S(1)} %get-tuple-element.17.ids, s32[8,8,128]{2,1,0:T(8,128)S(1)} %get-tuple-element.18.counts, f32[3,5,8,128]{3,2,1,0:T(8,128)S(1)} %get-tuple-element.19.sent, ...), custom_call_target="tpu_custom_call", output_to_operand_aliasing={{}: (0, {})} | custom-call | tf_op jit(solution)/shard_map/pallas_call | solution.py:469
  38.1 0.0 copy-start
  38.2 0.0 copy-start.1
  38.2 0.8 %shard_map.125.total = f32[4,64,512]{2,1,0:T(8,128)S(1)} custom-call(f32[4,64,512]{2,1,0:T(8,128)S(1)} %shard_map.124.steps, s32[7,1,1024]{2,1,0:T(1,128)S(1)} %get-tuple-element.17.ids, s32[8,8,128]{2,1,0:T(8,128)S(1)} %get-tuple-element.18.counts, f32[3,5,8,128]{3,2,1,0:T(8,128)S(1)} %get-tuple-element.19.sent, ...), custom_call_target="tpu_custom_call", output_to_operand_aliasing={{}: (0, {})} | custom-call | tf_op jit(solution)/shard_map/pallas_call | solution.py:469
  38.9 0.0 collective-permute-done.5.relayed
  39.0 0.2 copy-done
  39.1 0.0 copy-done.1
  39.2 3.2 %scatter_and_update.1 = (f32[64,512]{1,0:T(8,128)}, f32[3,64,512]{2,1,0:T(8,128)}) custom-call(f32[64,512]{1,0:T(8,128)S(1)} %bitcast.13, f32[3,64,512]{2,1,0:T(8,128)S(1)} %bitcast.11, f32[4,64,512]{2,1,0:T(8,128)S(1)} %shard_map.125.total, s32[7,1,1024]{2,1,0:T(1,128)S(1)} %get-tuple-element.17.ids, s32[8,8,128]{2,1,0:T(8,128)S(1)} %get-tuple-element.18.counts, ...), custom_call_target="tpu_custom_call" | custom-call | tf_op jit(solution)/shard_map/scatter_and_update/pallas_call | solution.py:480
  (3 shorter events, 0.0 us)
Async XLA Ops:
  7.7 7.2 %collective-permute-start = (f32[3,5,8,128]{3,2,1,0:T(8,128)S(1)}, f32[3,5,8,128]{3,2,1,0:T(8,128)S(1)}, u32[]{:S(2)}, u32[]{:S(2)}) collective-permute-start(f32[3,5,8,128]{3,2,1,0:T(8,128)S(1)} %get-tuple-element.19.sent), channel_id=1, source_target_pairs={{0,1},{1,0},{2,3},{3,2},{4,5},{5,4},{6,7},{7,6},{8,9},{9,8},{10,11... | collective-permute-start | bytes 184328 | tf_op jit(solution)/shard_map/ppermute | solution.py:423
  14.0 0.9 %collective-permute-start.2 = (f32[2,5,8,128]{3,2,1,0:T(8,128)S(1)}, f32[2,5,8,128]{3,2,1,0:T(8,128)S(1)}, u32[]{:S(2)}, u32[]{:S(2)}) collective-permute-start(f32[2,5,8,128]{3,2,1,0:T(8,128)S(1)} %get-tuple-element.25.rest), channel_id=1, source_target_pairs={{480,481},{481,480},{482,483},{483,482},{484,485},{485,484},{486,4... | collective-permute-start | bytes 122888 | tf_op jit(solution)/shard_map/ppermute | solution.py:437
  14.9 17.1 %collective-permute-start.3 = (f32[2,5,8,128]{3,2,1,0:T(8,128)S(1)}, f32[2,5,8,128]{3,2,1,0:T(8,128)S(1)}, u32[]{:S(2)}, u32[]{:S(2)}) collective-permute-start(f32[2,5,8,128]{3,2,1,0:T(8,128)S(1)} %get-tuple-element.26), channel_id=1, source_target_pairs={{0,4},{1,17},{2,6},{3,19},{4,0},{5,21},{6,2},{7,23},{8,12},{9,25},... | collective-permute-start | bytes 122888 | tf_op jit(solution)/shard_map/ppermute | solution.py:457
  17.0 15.0 %collective-permute-start.4 = (f32[2,5,8,128]{3,2,1,0:T(8,128)S(1)}, f32[2,5,8,128]{3,2,1,0:T(8,128)S(1)}, u32[]{:S(2)}, u32[]{:S(2)}) collective-permute-start(f32[2,5,8,128]{3,2,1,0:T(8,128)S(1)} %get-tuple-element.27), channel_id=1, source_target_pairs={{0,2},{1,9},{2,0},{3,11},{4,6},{5,13},{6,4},{7,15},{8,10},{9,1},{1... | collective-permute-start | bytes 122888 | tf_op jit(solution)/shard_map/ppermute | solution.py:457
  19.4 13.8 %collective-permute-start.1 = (f32[2,5,8,128]{3,2,1,0:T(8,128)S(1)}, f32[2,5,8,128]{3,2,1,0:T(8,128)S(1)}, u32[]{:S(2)}, u32[]{:S(2)}) collective-permute-start(f32[2,5,8,128]{3,2,1,0:T(8,128)S(1)} %pack_far.1), channel_id=1, source_target_pairs={{0,32},{1,481},{2,34},{3,483},{4,36},{5,485},{6,38},{7,487},{8,40}... | collective-permute-start | bytes 122888 | tf_op jit(solution)/shard_map/ppermute | solution.py:457
  33.1 5.8 %collective-permute-start.5 = (f32[4,5,8,128]{3,2,1,0:T(8,128)S(1)}, f32[4,5,8,128]{3,2,1,0:T(8,128)S(1)}, u32[]{:S(2)}, u32[]{:S(2)}) collective-permute-start(f32[4,5,8,128]{3,2,1,0:T(8,128)S(1)} %pack.1), channel_id=1, source_target_pairs={{0,1},{1,0},{2,3},{3,2},{4,5},{5,4},{6,7},{7,6},{8,9},{9,8},{10,11... | collective-permute-start | bytes 245768 | tf_op jit(solution)/shard_map/ppermute | solution.py:466
  38.1 1.0 %copy-start = (f32[1,1,3,64,512]{4,3,2,1,0:T(8,128)S(1)}, f32[1,1,3,64,512]{4,3,2,1,0:T(8,128)}, u32[]{:S(2)}) copy-start(f32[1,1,3,64,512]{4,3,2,1,0:T(8,128)} %param.12) | copy-start | bytes 1179652
  38.2 1.0 %copy-start.1 = (f32[1,1,64,512]{3,2,1,0:T(8,128)S(1)}, f32[1,1,64,512]{3,2,1,0:T(8,128)}, u32[]{:S(2)}) copy-start(f32[1,1,64,512]{3,2,1,0:T(8,128)} %param.11) | copy-start | bytes 393220
